TPU v7x, 256 devices: a whole 4x4x8 slice. The times are simulated.
256 devices in a mesh: lat: 2 (over x_hi), dp: 64 (over z, y, core), exp: 2 (over x_lo).
Axes of the slice: x: 4 (x_hi: 2, x_lo: 2; x = x_hi * 2 + x_lo), y: 4, z: 8, core: 2. Of those that a mesh axis runs over, the one named last changes fastest.
Arguments:
- images: bfloat16 [128, 32, 256, 192], P(('dp', 'exp'), 'lat'), may hold values from -6 to 6
- cotangent: bfloat16 [128, 32, 256, 192], P(('dp', 'exp'), 'lat'), may hold values from -0.0625 to 0.0625
- labels: int32 [128, 32, 2, 1], P(('dp', 'exp'), 'lat'), may hold values from 0 to 15; in each aligned block of 32 rows (0 to 31, 32 to 63, ..., all dimensions but the last counted through in order) at most 3 rows name the same one
- dw_kernel: float32 [7, 7, 192], replicated, may hold values from -0.875 to 0.875
- ln_gain: float32 [192], replicated, may hold values from 0.5 to 2
- w_expand: bfloat16 [192, 768], replicated, may hold values from -0.4375 to 0.4375
- w_reduce: bfloat16 [768, 192], replicated, may hold values from -0.21875 to 0.21875
- exp_in: bfloat16 [16, 192, 768], P('exp'), may hold values from -0.4375 to 0.4375
- exp_out: bfloat16 [16, 768, 192], P('exp'), may hold values from -0.21875 to 0.21875
Outputs:
- output: bfloat16 [128, 32, 256, 192], P(('dp', 'exp'), 'lat')
- grad_in: float32 [16, 192, 768], P('exp')
- grad_out: float32 [16, 768, 192], P('exp')
Inputs may be any that keep to these rules, and one draw needn't show every extreme that they name: `labels`: among the 32 row blocks of one device (aligned runs of 32 blocks in the order clip, row, block), no class is named more than 3 times, a bound that some block reaches.
All inputs are finite; a program needn't handle non-finite values.
Results may differ from a plain program's by a relative error of at most 0.0072.
Values may be sent and summed in bfloat16 or wider, within the bound.
A program may use at most 128 MiB of HBM per device.

v0:
```python
import jax
import jax.numpy as jnp
from jax import lax
from jax.sharding import PartitionSpec as P
from jax.experimental import pallas as pl
from jax.experimental.pallas import tpu as pltpu

EXPERTS = 16
BLOCK = 128
CAP = 3


def with_halo(block, sides, width):
    for axis, dim in sides:
        count = lax.axis_size(axis)
        forward = [(i, i + 1) for i in range(count - 1)]
        backward = [(target, source) for source, target in forward]
        low = lax.ppermute(
            lax.slice_in_dim(block, block.shape[dim] - width, None, axis=dim), axis, forward
        )
        high = lax.ppermute(lax.slice_in_dim(block, 0, width, axis=dim), axis, backward)
        block = jnp.concatenate([low, block, high], axis=dim)
    return block


def reduce_plan(lat_size, dp_size):
    dp_bits = dp_size.bit_length() - 1
    rest = list(range(1, dp_bits))
    other = rest[2:] + rest[:2] if len(rest) > 2 else rest
    plan = [("dp", 0, 0)] + [("dp", a, b) for a, b in zip(rest, other)]
    plan += [("lat", 0, 0)] * (lat_size.bit_length() - 1)
    return plan


def allreduce_kernel(plan, rows, in_ref, out_in, out_outt, *scratch):
    stages = len(plan)
    bufs = scratch[:stages]
    sums = scratch[stages:2 * stages]
    staged = scratch[2 * stages:3 * stages]
    gathered = scratch[3 * stages]
    rs_send, rs_recv, ag_send, ag_recv = scratch[3 * stages + 1:]
    lat = lax.axis_index("lat")
    dp = lax.axis_index("dp")
    ex = lax.axis_index("exp")
    core = dp % 2

    bits, partners = [], []
    for axis, b0, b1 in plan:
        me = dp if axis == "dp" else lat
        bit = jnp.where(core == 0, (me // (1 << b0)) % 2, (me // (1 << b1)) % 2)
        step = jnp.where(core == 0, 1 << b0, 1 << b1)
        other = me + (1 - 2 * bit) * step
        bits.append(bit)
        partners.append((lat, other, ex) if axis == "dp" else (other, dp, ex))

    barrier = pltpu.get_barrier_semaphore()
    for dev in partners:
        pl.semaphore_signal(barrier, 1, device_id=dev, device_id_type=pl.DeviceIdType.MESH)
    pl.semaphore_wait(barrier, stages)

    def chunked(count, body):
        chunk = min(count, 1152)
        lax.fori_loop(0, count // chunk, lambda i, c: (body(pl.multiple_of(i * chunk, 16), chunk), c)[1], 0)

    los = []
    lo = jnp.int32(0)
    for k in range(stages):
        half = rows >> (k + 1)
        los.append(lo)
        src = in_ref if k == 0 else sums[k - 1]
        keep = bits[k] * half
        give = (1 - bits[k]) * half

        def narrow(at, chunk, src=src, give=give, k=k):
            staged[k][pl.ds(at, chunk)] = src[pl.ds(pl.multiple_of(give + at, 16), chunk)].astype(jnp.bfloat16)

        chunked(half, narrow)
        copy = pltpu.make_async_remote_copy(
            src_ref=staged[k],
            dst_ref=bufs[k],
            send_sem=rs_send.at[k],
            recv_sem=rs_recv.at[k],
            device_id=partners[k],
            device_id_type=pl.DeviceIdType.MESH,
        )
        copy.start()
        copy.wait()

        def add(at, chunk, src=src, keep=keep, k=k):
            sums[k][pl.ds(at, chunk)] = src[pl.ds(pl.multiple_of(keep + at, 16), chunk)] + bufs[k][
                pl.ds(at, chunk)
            ].astype(jnp.float32)

        chunked(half, add)
        lo = lo + bits[k] * half

    last = rows >> stages
    lo = pl.multiple_of(lo, 16)
    gathered[pl.ds(lo, last)] = sums[stages - 1][...].astype(jnp.bfloat16)
    for k in reversed(range(stages)):
        half = rows >> (k + 1)
        copy = pltpu.make_async_remote_copy(
            src_ref=gathered.at[pl.ds(pl.multiple_of(lo, 16), half)],
            dst_ref=gathered.at[pl.ds(pl.multiple_of(lo, 16), half)],
            send_sem=ag_send.at[k],
            recv_sem=ag_recv.at[k],
            device_id=partners[k],
            device_id_type=pl.DeviceIdType.MESH,
        )
        copy.start()
        copy.wait()
        lo = los[k]

    experts, channels, hidden = out_in.shape
    pieces = hidden // 128
    for e in range(experts):
        for t, dst in enumerate((out_in, out_outt)):
            for c in range(pieces):
                at = ((e * 2 + t) * pieces + c) * channels
                dst[e, :, c * 128:(c + 1) * 128] = gathered[at:at + channels].astype(jnp.float32)


def tree_allreduce(flat, experts, channels, hidden):
    rows = flat.shape[0]
    plan = reduce_plan(lax.axis_size("lat"), lax.axis_size("dp"))
    stages = len(plan)
    scratch = [pltpu.VMEM((rows >> (k + 1), 128), jnp.bfloat16) for k in range(stages)]
    scratch += [pltpu.VMEM((rows >> (k + 1), 128), jnp.float32) for k in range(stages)]
    scratch += [pltpu.VMEM((rows >> (k + 1), 128), jnp.bfloat16) for k in range(stages)]
    scratch += [pltpu.VMEM((rows, 128), jnp.bfloat16)]
    scratch += [pltpu.SemaphoreType.DMA((stages,))] * 4
    return pl.pallas_call(
        lambda *refs: allreduce_kernel(plan, rows, *refs),
        out_shape=[jax.ShapeDtypeStruct((experts, channels, hidden), jnp.float32)] * 2,
        in_specs=[pl.BlockSpec(memory_space=pltpu.VMEM)],
        out_specs=[pl.BlockSpec(memory_space=pltpu.VMEM)] * 2,
        scratch_shapes=scratch,
        compiler_params=pltpu.CompilerParams(
            collective_id=0, has_side_effects=True, vmem_limit_bytes=62 * 1024 * 1024
        ),
    )(flat)

def expert_kernel(x_ref, g_ref, win_ref, wout_ref, out_ref, flat_ref):
    x = x_ref[...]
    g = g_ref[...]
    w_out = wout_ref[...]
    pre = jnp.dot(x, win_ref[...], preferred_element_type=jnp.float32)
    cdf = 0.5 * (1.0 + lax.erf(pre * 0.7071067811865476))
    hidden = (pre * cdf).astype(jnp.bfloat16)
    out_ref[...] = jnp.dot(hidden, w_out, preferred_element_type=jnp.float32).astype(out_ref.dtype)
    grad_out_t = lax.dot_general(g, hidden, (((0,), (0,)), ((), ())), preferred_element_type=jnp.float32)
    back = lax.dot_general(g, w_out, (((1,), (1,)), ((), ())), preferred_element_type=jnp.float32)
    slope = cdf + pre * jnp.exp(-0.5 * pre * pre) * 0.3989422804014327
    scaled = (back * slope).astype(jnp.bfloat16)
    grad_in = lax.dot_general(x, scaled, (((0,), (0,)), ((), ())), preferred_element_type=jnp.float32)
    for c in range(grad_in.shape[1] // 128):
        flat_ref[0, c] = grad_in[:, c * 128:(c + 1) * 128]
        flat_ref[1, c] = grad_out_t[:, c * 128:(c + 1) * 128]


def run_experts(inputs, grads, w_in, w_out):
    experts, tokens, channels = inputs.shape
    hidden = w_in.shape[2]
    pieces = hidden // 128
    tok = pl.BlockSpec((None, tokens, channels), lambda e: (e, 0, 0))
    return pl.pallas_call(
        expert_kernel,
        grid=(experts,),
        out_shape=[
            jax.ShapeDtypeStruct((experts, tokens, channels), jnp.bfloat16),
            jax.ShapeDtypeStruct((experts, 2, pieces, channels, 128), jnp.float32),
        ],
        in_specs=[
            tok,
            tok,
            pl.BlockSpec((None, channels, hidden), lambda e: (e, 0, 0)),
            pl.BlockSpec((None, hidden, channels), lambda e: (e, 0, 0)),
        ],
        out_specs=[tok, pl.BlockSpec((None, 2, pieces, channels, 128), lambda e: (e, 0, 0, 0, 0))],
        compiler_params=pltpu.CompilerParams(vmem_limit_bytes=48 * 1024 * 1024),
    )(inputs, grads, w_in, w_out)


def gelu_slope(values):
    return (
        0.5 * (1.0 + lax.erf(values * 0.7071067811865476))
        + values * jnp.exp(-0.5 * values * values) * 0.3989422804014327
    )


def depthwise(padded, kernel):
    row_count = padded.shape[1] - 6
    col_count = padded.shape[2] - 6
    summed = jnp.zeros((padded.shape[0], row_count, col_count, padded.shape[3]), jnp.float32)
    for row_off in range(7):
        for col_off in range(7):
            window = padded[:, row_off : row_off + row_count, col_off : col_off + col_count, :]
            summed = summed + window.astype(jnp.float32) * kernel[row_off, col_off]
    return summed


def widen(picture):
    return jnp.pad(picture, ((0, 0), (0, 0), (3, 3), (0, 0)))


def dense_block(images, smoothed, ln_gain, w_expand, w_reduce):
    channels = images.shape[-1]
    channel_mean = jnp.mean(smoothed, axis=-1, keepdims=True)
    centered = smoothed - channel_mean
    variance = jnp.mean(centered * centered, axis=-1, keepdims=True)
    normed = (centered * lax.rsqrt(variance + 1e-06) * ln_gain).astype(jnp.bfloat16)
    flat_normed = normed.reshape(-1, channels)
    expanded = jnp.dot(flat_normed, w_expand, preferred_element_type=jnp.float32)
    active = jax.nn.gelu(expanded, approximate=False).astype(jnp.bfloat16)
    reduced = jnp.dot(active, w_reduce, preferred_element_type=jnp.float32)
    dense_out = images.reshape(-1, channels).astype(jnp.float32) + reduced
    return dense_out.astype(jnp.bfloat16).reshape(images.shape)


def expert_pass(inputs, grads_in, w_in, w_out):
    pre_act = jnp.dot(inputs, w_in, preferred_element_type=jnp.float32)
    hidden = jax.nn.gelu(pre_act, approximate=False).astype(jnp.bfloat16)
    outputs = jnp.dot(hidden, w_out, preferred_element_type=jnp.float32).astype(jnp.bfloat16)
    grad_out = jnp.dot(hidden.T, grads_in, preferred_element_type=jnp.float32)
    back_prop = jnp.dot(grads_in, w_out.T, preferred_element_type=jnp.float32)
    scaled = (back_prop * gelu_slope(pre_act)).astype(jnp.bfloat16)
    grad_in = jnp.dot(inputs.T, scaled, preferred_element_type=jnp.float32)
    return (outputs, grad_in, grad_out)


def body(images, cotangent, labels, dw_kernel, ln_gain, w_expand, w_reduce, exp_in, exp_out):
    channels = images.shape[-1]
    padded = with_halo(images, (("lat", 1),), 3)
    smoothed = depthwise(widen(padded), dw_kernel)
    dense_out = dense_block(images, smoothed, ln_gain, w_expand, w_reduce)
    blocks = dense_out.reshape(-1, BLOCK, channels)
    grad_blocks = cotangent.reshape(-1, BLOCK, channels)
    flat_labels = labels.reshape(-1)
    members = (flat_labels[:, None] == jnp.arange(EXPERTS, dtype=jnp.int32)[None, :]).astype(
        jnp.int32
    )
    before = jnp.sum(jnp.cumsum(members, axis=0) * members, axis=1) - 1
    slot_of = flat_labels * CAP + before
    placer = jnp.arange(EXPERTS * CAP, dtype=jnp.int32)[:, None] == slot_of[None, :]
    block_of_slot = jnp.argmax(placer, axis=1)
    filled = jnp.any(placer, axis=1)[:, None, None]
    outgoing = blocks[block_of_slot].reshape(EXPERTS, CAP, BLOCK, channels)
    outgoing_grads = jnp.where(filled, grad_blocks[block_of_slot], jnp.zeros((), jnp.bfloat16)).reshape(
        EXPERTS, CAP, BLOCK, channels
    )
    arrived, arrived_grads = (
        lax.all_to_all(outgoing, "exp", split_axis=0, concat_axis=1, tiled=True),
        lax.all_to_all(outgoing_grads, "exp", split_axis=0, concat_axis=1, tiled=True),
    )
    local = arrived.shape[0]
    results, flat = run_experts(
        arrived.reshape(local, -1, channels), arrived_grads.reshape(local, -1, channels), exp_in, exp_out
    )
    returned = lax.all_to_all(results.reshape(arrived.shape), "exp", split_axis=1, concat_axis=0, tiled=True)
    grad_in, grad_out_t = tree_allreduce(flat.reshape(-1, 128), local, channels, exp_in.shape[2])
    grad_out = jnp.transpose(grad_out_t, (0, 2, 1))
    expert_out = returned.reshape(EXPERTS * CAP, BLOCK, channels)[slot_of]
    output = (
        dense_out.astype(jnp.float32) + expert_out.reshape(dense_out.shape).astype(jnp.float32)
    ).astype(jnp.bfloat16)
    return (output, grad_in, grad_out)


def solution(mesh):
    in_specs = (
        P(("dp", "exp"), "lat", None, None),
        P(("dp", "exp"), "lat", None, None),
        P(("dp", "exp"), "lat", None, None),
        P(),
        P(),
        P(),
        P(),
        P("exp", None, None),
        P("exp", None, None),
    )
    out_specs = (P(("dp", "exp"), "lat", None, None), P("exp", None, None), P("exp", None, None))
    return jax.shard_map(body, mesh=mesh, in_specs=in_specs, out_specs=out_specs, check_vma=False)
```

profile of v0, /device:TPU:7, one launch (start us, length us, event | category | flops | bytes accessed | tf_op | source)
XLA Modules:
  0.0 324.4 jit_solution(17573616162430382046)
XLA Ops:
  0.6 1.1 fusion.61
  1.8 1.3 collective-permute-start
  3.1 5.5 %collective-permute-start.1 = (bf16[1,3,256,192]{2,3,1,0:T(8,128)(2,1)S(1)}, bf16[1,3,256,192]{2,3,1,0:T(8,128)(2,1)S(1)}, u32[]{:S(2)}, u32[]{:S(2)}) collective-permute-start(bf16[1,3,256,192]{2,3,1,0:T(8,128)(2,1)S(1)} %get-tuple-element.31), channel_id=1, source_target_pairs={{128,0},{129,1},{130,2},{131,3},{132,4},{133,5},{134,6},{135,7},{1... | collective-permute-start | bytes 884744 | tf_op jit(solution)/shard_map/ppermute | solution.py:21
  8.6 0.7 broadcast_multiply_fusion.1
  9.3 0.8 copy.60
  10.1 0.1 reshape.298
  10.3 0.2 select_reduce_fusion
  10.5 0.1 fusion.28
  10.6 0.6 iota_reduce_fusion
  11.3 0.1 mul.713
  11.4 0.1 broadcast_in_dim.17
  11.5 2.3 copy.63
  13.8 2.0 reshape.301
  15.7 2.0 copy.64
  17.7 2.3 gather_fusion.1
  20.1 3.3 %broadcast_select_fusion = bf16[16,3,128,192]{2,3,1,0:T(8,128)(2,1)} fusion(bf16[16,3,128,192]{2,3,1,0:T(8,128)(2,1)} %bitcast.117, pred[16,3]{1,0:T(8,128)(4,1)S(1)} %broadcast_in_dim.17), kind=kLoop, calls=%fused_computation.39 | loop fusion | flops 1179648 | bytes 4718640 | tf_op jit(solution)/shard_map/jit(_where)/select_n | solution.py:248
  23.4 5.6 %all-to-all-start.1 = ((bf16[16,3,128,192]{2,3,1,0:T(8,128)(2,1)}), bf16[16,3,128,192]{2,3,1,0:T(8,128)(2,1)}, u32[]{:S(2)}, u32[]{:S(2)}) async-start(bf16[16,3,128,192]{2,3,1,0:T(8,128)(2,1)} %broadcast_select_fusion), calls=%async_computation.1 | async-start | bytes 4718592 | tf_op jit(solution)/shard_map/all_to_all | solution.py:253
  29.1 0.7 constant_dynamic-update-slice_fusion
  29.7 2.1 copy.75
  31.8 2.2 fusion.25
  34.1 26.9 %fusion.60 = (f32[16,256]{1,0:T(8,128)S(1)}, f32[1,16,256,192]{2,3,1,0:T(8,128)S(1)}) fusion(f32[192]{0:T(256)S(1)} %bitcast.158, bf16[1,22,262,192]{2,3,1,0:T(8,128)(2,1)S(1)} %fusion.25, f32[192]{0:T(256)S(1)} %bitcast.159, f32[192]{0:T(256)S(1)} %bitcast.131, f32[192]{0:T(256)S(1)} %bitcast.132, ...), kind=kLoop, calls=%fused_computation.91 | loop fusion | flops 115601408 | bytes 80270080 | tf_op jit(solution)/shard_map/reduce_sum | solution.py:208
  61.0 0.3 multiply_reduce_fusion
  61.4 0.3 copy-done.6
  61.7 0.5 fusion.66
  62.2 0.2 copy.76
  62.4 0.2 copy-done.7
  62.6 32.4 %fusion.65 = (f32[4096,192]{0,1:T(8,128)}, bf16[4096,192]{0,1:T(8,128)(2,1)}) fusion(f32[4096,192]{0,1:T(8,128)} %bitcast.127, bf16[768,192]{0,1:T(8,128)(2,1)S(1)} %copy-done, bf16[4096,192]{0,1:T(8,128)(2,1)S(1)} %bitcast.129, bf16[192,768]{1,0:T(8,128)(2,1)S(1)} %copy-done.7), kind=kOutput, calls=%fused_computation.96 | convolution fusion | flops 2622750720 | bytes 10027008 | tf_op jit(solution)/shard_map/dot_general | solution.py:215
  95.0 1.8 copy_bitcast_fusion
  96.9 2.3 gather_fusion
  99.2 3.8 %all-to-all-start = ((bf16[16,3,128,192]{2,3,1,0:T(8,128)(2,1)}), bf16[16,3,128,192]{2,3,1,0:T(8,128)(2,1)S(1)}, u32[]{:S(2)}, u32[]{:S(2)}) async-start(bf16[16,3,128,192]{2,3,1,0:T(8,128)(2,1)} %bitcast.116), calls=%async_computation | async-start | bytes 4718592 | tf_op jit(solution)/shard_map/all_to_all | solution.py:252
  103.1 4.5 %copy.66.wout_ref = bf16[8,768,192]{2,1,0:T(8,128)(2,1)} copy(bf16[8,768,192]{1,2,0:T(8,128)(2,1)} %param.17) | data formatting | bytes 4718592 | tf_op args[8]
  107.6 4.5 %copy.65 = bf16[8,2,3,128,192]{4,3,2,1,0:T(8,128)(2,1)} copy(bf16[8,2,3,128,192]{3,4,2,0,1:T(8,128)(2,1)} %bitcast.55) | data formatting | bytes 4718592 | tf_op jit(solution)/shard_map/all_to_all | solution.py:253
  112.1 16.2 %all-to-all-done = bf16[16,3,128,192]{2,3,1,0:T(8,128)(2,1)S(1)} async-done(((bf16[16,3,128,192]{2,3,1,0:T(8,128)(2,1)}), bf16[16,3,128,192]{2,3,1,0:T(8,128)(2,1)S(1)}, u32[]{:S(2)}, u32[]{:S(2)}) %all-to-all-start) | async-done | bytes 2359328 | tf_op jit(solution)/shard_map/all_to_all | solution.py:252
  128.3 2.7 copy.62
  131.0 1.7 copy-done.2
  132.7 16.2 %shard_map.112 = (bf16[8,768,192]{2,1,0:T(8,128)(2,1)S(1)}, f32[8,2,6,192,128]{4,3,2,1,0:T(8,128)}) custom-call(bf16[8,768,192]{2,1,0:T(8,128)(2,1)} %bitcast.120, bf16[8,768,192]{2,1,0:T(8,128)(2,1)} %bitcast.119, bf16[8,192,768]{2,1,0:T(8,128)(2,1)S(1)} %copy-done.2, bf16[8,768,192]{2,1,0:T(8,128)(2,1)} %copy.66.wout_ref), custom_call_target="tpu_custom_call" | custom-call | tf_op jit(solution)/shard_map/pallas_call | solution.py:166
  148.9 2.7 copy.67
  151.6 6.3 %all-to-all-start.2 = ((bf16[8,6,128,192]{2,3,0,1:T(8,128)(2,1)}), bf16[8,6,128,192]{2,3,0,1:T(8,128)(2,1)}, u32[]{:S(2)}, u32[]{:S(2)}) async-start(bf16[8,6,128,192]{2,3,0,1:T(8,128)(2,1)} %copy.67), calls=%async_computation.2 | async-start | bytes 4718592 | tf_op jit(solution)/shard_map/all_to_all | solution.py:259
  157.9 2.9 copy.77
  160.8 142.7 %shard_map.113 = (f32[8,192,768]{2,1,0:T(8,128)}, f32[8,192,768]{2,1,0:T(8,128)}) custom-call(f32[18432,128]{1,0:T(8,128)} %bitcast.121), custom_call_target="tpu_custom_call" | custom-call | tf_op jit(solution)/shard_map/pallas_call | solution.py:132
  303.5 1.8 copy.69
  305.4 1.9 gather_fusion.2
  307.3 2.3 copy.71
  309.6 2.5 reshape.308
  312.1 3.4 %fusion.26 = bf16[1,16,256,192]{2,1,3,0:T(8,128)(2,1)S(1)} fusion(f32[1,16,256,192]{2,1,3,0:T(8,128)} %reshape.308, f32[24,8,16,256]{3,2,1,0:T(8,128)} %copy.77), kind=kLoop, calls=%fused_computation.35 | loop fusion | flops 1572864 | bytes 7864320 | tf_op jit(solution)/shard_map/convert_element_type | solution.py:265
  315.5 1.7 copy.72
  317.2 5.0 %copy.85 = f32[8,192,768]{2,1,0:T(8,128)} copy(f32[8,192,768]{2,1,0:T(8,128)} %get-tuple-element.89) | data formatting | bytes 9437184
  322.2 2.2 copy.86
  (36 shorter events, 0.4 us)
Async XLA Ops:
  0.6 61.8 %copy-start = (bf16[768,192]{0,1:T(8,128)(2,1)S(1)}, bf16[768,192]{0,1:T(8,128)(2,1)}, u32[]{:S(2)}) copy-start(bf16[768,192]{0,1:T(8,128)(2,1)} %param.15) | copy-start | bytes 884740
  1.8 27.2 %collective-permute-start = (bf16[1,3,256,192]{2,3,1,0:T(8,128)(2,1)S(1)}, bf16[1,3,256,192]{2,3,1,0:T(8,128)(2,1)S(1)}, u32[]{:S(2)}, u32[]{:S(2)}) collective-permute-start(bf16[1,3,256,192]{2,3,1,0:T(8,128)(2,1)S(1)} %get-tuple-element.30), channel_id=1, source_target_pairs={{0,128},{1,129},{2,130},{3,131},{4,132},{5,133},{6,134},{7,135},{8... | collective-permute-start | bytes 884744 | tf_op jit(solution)/shard_map/ppermute | solution.py:18
  3.1 28.7 %collective-permute-start.1 = (bf16[1,3,256,192]{2,3,1,0:T(8,128)(2,1)S(1)}, bf16[1,3,256,192]{2,3,1,0:T(8,128)(2,1)S(1)}, u32[]{:S(2)}, u32[]{:S(2)}) collective-permute-start(bf16[1,3,256,192]{2,3,1,0:T(8,128)(2,1)S(1)} %get-tuple-element.31), channel_id=1, source_target_pairs={{128,0},{129,1},{130,2},{131,3},{132,4},{133,5},{134,6},{135,7},{1... | collective-permute-start | bytes 884744 | tf_op jit(solution)/shard_map/ppermute | solution.py:21
  23.4 5.6 %copy-start.5 = (f32[7,7,192]{2,1,0:T(8,128)S(1)}, f32[7,7,192]{2,1,0:T(8,128)}, u32[]{:S(2)}) copy-start(f32[7,7,192]{2,1,0:T(8,128)} %param.12) | copy-start | bytes 112900
  23.4 5.7 %copy-start.3 = (bf16[1,16,256,192]{2,3,1,0:T(8,128)(2,1)S(1)}, bf16[1,16,256,192]{2,3,1,0:T(8,128)(2,1)}, u32[]{:S(2)}) copy-start(bf16[1,16,256,192]{2,3,1,0:T(8,128)(2,1)} %param.9) | copy-start | bytes 4718596
  23.4 75.8 %all-to-all-start.1 = ((bf16[16,3,128,192]{2,3,1,0:T(8,128)(2,1)}), bf16[16,3,128,192]{2,3,1,0:T(8,128)(2,1)}, u32[]{:S(2)}, u32[]{:S(2)}) async-start(bf16[16,3,128,192]{2,3,1,0:T(8,128)(2,1)} %broadcast_select_fusion), calls=%async_computation.1 | async-start | bytes 4718592 | tf_op jit(solution)/shard_map/all_to_all | solution.py:253
  61.0 0.7 copy-start.6
  61.7 1.0 copy-start.7
  99.2 29.1 %all-to-all-start = ((bf16[16,3,128,192]{2,3,1,0:T(8,128)(2,1)}), bf16[16,3,128,192]{2,3,1,0:T(8,128)(2,1)S(1)}, u32[]{:S(2)}, u32[]{:S(2)}) async-start(bf16[16,3,128,192]{2,3,1,0:T(8,128)(2,1)} %bitcast.116), calls=%async_computation | async-start | bytes 4718592 | tf_op jit(solution)/shard_map/all_to_all | solution.py:252
  131.0 1.7 copy-start.2
  151.6 6.3 %copy-start.4 = (f32[4096,192]{0,1:T(8,128)S(1)}, f32[4096,192]{0,1:T(8,128)}, u32[]{:S(2)}) copy-start(f32[4096,192]{0,1:T(8,128)} %get-tuple-element.81) | copy-start | bytes 9437188
  151.6 151.9 %all-to-all-start.2 = ((bf16[8,6,128,192]{2,3,0,1:T(8,128)(2,1)}), bf16[8,6,128,192]{2,3,0,1:T(8,128)(2,1)}, u32[]{:S(2)}, u32[]{:S(2)}) async-start(bf16[8,6,128,192]{2,3,0,1:T(8,128)(2,1)} %copy.67), calls=%async_computation.2 | async-start | bytes 4718592 | tf_op jit(solution)/shard_map/all_to_all | solution.py:259
  315.5 6.7 %slice-start = ((s8[4718592]{0:T(1024)(128)(4,1)}), s8[524288]{0:T(1024)(128)(4,1)S(1)}, s32[]{:S(2)}) async-start(s8[4718592]{0:T(1024)(128)(4,1)} %bitcast.124), calls=%async_computation.3 | async-start | bytes 1048576
  317.2 5.0 %slice-start.1 = ((s8[4718592]{0:T(1024)(128)(4,1)}), s8[4194304]{0:T(1024)(128)(4,1)S(1)}, s32[]{:S(2)}) async-start(s8[4718592]{0:T(1024)(128)(4,1)} %bitcast.124), calls=%async_computation.4 | async-start | bytes 8388608
  317.2 7.2 %copy-start.1 = (bf16[768,192]{0,1:T(8,128)(2,1)S(1)}, bf16[768,192]{0,1:T(8,128)(2,1)}, u32[]{:S(2)}) copy-start(bf16[768,192]{0,1:T(8,128)(2,1)} %param.15) | copy-start | bytes 884740
where the time goes:
time: 326 us; the launch traced here: 324 us
  Pallas kernels  159 us (49%)
  local copies, waits for them, and re-layouts  54.3 us (17%)
  other arithmetic  39.1 us (12%)
  matrix products  32.4 us (10%)
  starting transfers between devices  22.6 us (7%)
  waiting for transfers between devices  16.2 us (5%)
    pallas_call x1, Pallas kernels, tree_allreduce(): pl.pallas_call(lambda *refs: allreduce_kernel(plan, rows, *refs), out_sha...  143 us
    dot_general x1, matrix products, dense_block(): reduced = jnp.dot(active, w_reduce, preferred_element_type=jnp.float32)  32.4 us
    reduce_sum x1, other arithmetic, dense_block(): channel_mean = jnp.mean(smoothed, axis=-1, keepdims=True)  26.9 us
    unnamed x30, local copies, waits for them, and re-layouts  23.8 us
    all_to_all x1, waiting for transfers between devices, body(): lax.all_to_all(outgoing, 'exp', split_axis=0, concat_axis=1, tiled=True)  16.2 us
    pallas_call x1, Pallas kernels, run_experts(): pl.pallas_call(expert_kernel, grid=(experts,), out_shape=[jax.ShapeDtypeS...  16.2 us
  transfers between devices with their start and end apart: 5, of which 1 were waited for; matrix products, arithmetic and copies ran while one was open for 30% of the time, Pallas kernels for 44%

commit v1 on v0

--- a/solution.py
+++ b/solution.py
@@ -141,45 +141,45 @@
     )(flat)
 
 def expert_kernel(x_ref, g_ref, win_ref, wout_ref, out_ref, flat_ref):
-    x = x_ref[...]
-    g = g_ref[...]
-    w_out = wout_ref[...]
-    pre = jnp.dot(x, win_ref[...], preferred_element_type=jnp.float32)
+    slots = x_ref.shape[0]
+    x_t = jnp.concatenate([x_ref[s] for s in range(slots)], axis=1)
+    g_t = jnp.concatenate([g_ref[s] for s in range(slots)], axis=1)
+    w_out_t = wout_ref[...]
+    pre = lax.dot_general(x_t, win_ref[...], (((0,), (0,)), ((), ())), preferred_element_type=jnp.float32)
     cdf = 0.5 * (1.0 + lax.erf(pre * 0.7071067811865476))
     hidden = (pre * cdf).astype(jnp.bfloat16)
-    out_ref[...] = jnp.dot(hidden, w_out, preferred_element_type=jnp.float32).astype(out_ref.dtype)
-    grad_out_t = lax.dot_general(g, hidden, (((0,), (0,)), ((), ())), preferred_element_type=jnp.float32)
-    back = lax.dot_general(g, w_out, (((1,), (1,)), ((), ())), preferred_element_type=jnp.float32)
+    out_t = lax.dot_general(w_out_t, hidden, (((1,), (1,)), ((), ())), preferred_element_type=jnp.float32)
+    out_t = out_t.astype(out_ref.dtype)
+    width = out_ref.shape[2]
+    for s in range(slots):
+        out_ref[s] = out_t[:, s * width:(s + 1) * width]
+    grad_out_t = jnp.dot(g_t, hidden, preferred_element_type=jnp.float32)
+    back = lax.dot_general(g_t, w_out_t, (((0,), (0,)), ((), ())), preferred_element_type=jnp.float32)
     slope = cdf + pre * jnp.exp(-0.5 * pre * pre) * 0.3989422804014327
     scaled = (back * slope).astype(jnp.bfloat16)
-    grad_in = lax.dot_general(x, scaled, (((0,), (0,)), ((), ())), preferred_element_type=jnp.float32)
+    grad_in = jnp.dot(x_t, scaled, preferred_element_type=jnp.float32)
     for c in range(grad_in.shape[1] // 128):
         flat_ref[0, c] = grad_in[:, c * 128:(c + 1) * 128]
         flat_ref[1, c] = grad_out_t[:, c * 128:(c + 1) * 128]
 
 
-def run_experts(inputs, grads, w_in, w_out):
-    experts, tokens, channels = inputs.shape
+def run_experts(inputs, grads, w_in, w_out_t):
+    experts, slots, channels, width = inputs.shape
     hidden = w_in.shape[2]
     pieces = hidden // 128
-    tok = pl.BlockSpec((None, tokens, channels), lambda e: (e, 0, 0))
+    tok = pl.BlockSpec((None, slots, channels, width), lambda e: (e, 0, 0, 0))
+    weight = pl.BlockSpec((None, channels, hidden), lambda e: (e, 0, 0))
     return pl.pallas_call(
         expert_kernel,
         grid=(experts,),
         out_shape=[
-            jax.ShapeDtypeStruct((experts, tokens, channels), jnp.bfloat16),
+            jax.ShapeDtypeStruct(inputs.shape, jnp.bfloat16),
             jax.ShapeDtypeStruct((experts, 2, pieces, channels, 128), jnp.float32),
         ],
-        in_specs=[
-            tok,
-            tok,
-            pl.BlockSpec((None, channels, hidden), lambda e: (e, 0, 0)),
-            pl.BlockSpec((None, hidden, channels), lambda e: (e, 0, 0)),
-        ],
+        in_specs=[tok, tok, weight, weight],
         out_specs=[tok, pl.BlockSpec((None, 2, pieces, channels, 128), lambda e: (e, 0, 0, 0, 0))],
         compiler_params=pltpu.CompilerParams(vmem_limit_bytes=48 * 1024 * 1024),
-    )(inputs, grads, w_in, w_out)
-
+    )(inputs, grads, w_in, w_out_t)
 
 def gelu_slope(values):
     return (
@@ -233,8 +233,15 @@
     padded = with_halo(images, (("lat", 1),), 3)
     smoothed = depthwise(widen(padded), dw_kernel)
     dense_out = dense_block(images, smoothed, ln_gain, w_expand, w_reduce)
-    blocks = dense_out.reshape(-1, BLOCK, channels)
-    grad_blocks = cotangent.reshape(-1, BLOCK, channels)
+    rows, width = images.shape[1], images.shape[2]
+    per_row = width // BLOCK
+
+    def to_blocks(pixels):
+        pixels = pixels.reshape(rows, per_row, BLOCK, channels)
+        return jnp.transpose(pixels, (0, 1, 3, 2)).reshape(rows * per_row, channels, BLOCK)
+
+    blocks = to_blocks(dense_out)
+    grad_blocks = to_blocks(cotangent)
     flat_labels = labels.reshape(-1)
     members = (flat_labels[:, None] == jnp.arange(EXPERTS, dtype=jnp.int32)[None, :]).astype(
         jnp.int32
@@ -244,22 +251,21 @@
     placer = jnp.arange(EXPERTS * CAP, dtype=jnp.int32)[:, None] == slot_of[None, :]
     block_of_slot = jnp.argmax(placer, axis=1)
     filled = jnp.any(placer, axis=1)[:, None, None]
-    outgoing = blocks[block_of_slot].reshape(EXPERTS, CAP, BLOCK, channels)
+    outgoing = blocks[block_of_slot].reshape(EXPERTS, CAP, channels, BLOCK)
     outgoing_grads = jnp.where(filled, grad_blocks[block_of_slot], jnp.zeros((), jnp.bfloat16)).reshape(
-        EXPERTS, CAP, BLOCK, channels
+        EXPERTS, CAP, channels, BLOCK
     )
     arrived, arrived_grads = (
         lax.all_to_all(outgoing, "exp", split_axis=0, concat_axis=1, tiled=True),
         lax.all_to_all(outgoing_grads, "exp", split_axis=0, concat_axis=1, tiled=True),
     )
     local = arrived.shape[0]
-    results, flat = run_experts(
-        arrived.reshape(local, -1, channels), arrived_grads.reshape(local, -1, channels), exp_in, exp_out
-    )
-    returned = lax.all_to_all(results.reshape(arrived.shape), "exp", split_axis=1, concat_axis=0, tiled=True)
+    results, flat = run_experts(arrived, arrived_grads, exp_in, jnp.transpose(exp_out, (0, 2, 1)))
+    returned = lax.all_to_all(results, "exp", split_axis=1, concat_axis=0, tiled=True)
     grad_in, grad_out_t = tree_allreduce(flat.reshape(-1, 128), local, channels, exp_in.shape[2])
     grad_out = jnp.transpose(grad_out_t, (0, 2, 1))
-    expert_out = returned.reshape(EXPERTS * CAP, BLOCK, channels)[slot_of]
+    expert_blocks = returned.reshape(EXPERTS * CAP, channels, BLOCK)[slot_of]
+    expert_out = jnp.transpose(expert_blocks.reshape(rows, per_row, channels, BLOCK), (0, 1, 3, 2))
     output = (
         dense_out.astype(jnp.float32) + expert_out.reshape(dense_out.shape).astype(jnp.float32)
     ).astype(jnp.bfloat16)

time: 326 us -> 325 us (level)
  local copies, waits for them, and re-layouts: 54.3 us -> 43.1 us
  waiting for transfers between devices: 16.2 us -> 22 us
  other arithmetic: 39.1 us -> 43.4 us
    unnamed x30 -> x25, local copies, waits for them, and re-layouts: 23.8 us -> 13.3 us
    all_to_all x1, waiting for transfers between devices: 16.2 us -> 22 us  [body(): lax.all_to_all(outgoing, 'exp', split_axis=0, concat_axis=1, tiled=True)]
    reshape x3 -> x1, local copies, waits for them, and re-layouts: 6.65 us -> 3.5 us  [to_blocks(): pixels = pixels.reshape(rows, per_row, BLOCK, channels)]
  transfers between devices with their start and end apart: 5 -> 5, of which waited for: 1 -> 1; matrix products, arithmetic and copies ran while one was open for 30% -> 28% of each run, Pallas kernels for 44% -> 44%
where the time goes in v1:
time: 325 us
  Pallas kernels  160 us (49%)
  other arithmetic  43.4 us (13%)
  local copies, waits for them, and re-layouts  43.1 us (13%)
  matrix products  32.6 us (10%)
  starting transfers between devices  22.5 us (7%)
  waiting for transfers between devices  22 us (7%)
    pallas_call x1, Pallas kernels, tree_allreduce(): pl.pallas_call(lambda *refs: allreduce_kernel(plan, rows, *refs), out_sha...  143 us
    dot_general x1, matrix products, dense_block(): reduced = jnp.dot(active, w_reduce, preferred_element_type=jnp.float32)  32.6 us
    reduce_sum x1, other arithmetic, dense_block(): channel_mean = jnp.mean(smoothed, axis=-1, keepdims=True)  26.9 us
    all_to_all x1, waiting for transfers between devices, body(): lax.all_to_all(outgoing, 'exp', split_axis=0, concat_axis=1, tiled=True)  22 us
    pallas_call x1, Pallas kernels, run_experts(): pl.pallas_call(expert_kernel, grid=(experts,), out_shape=[jax.ShapeDtypeS...  17.3 us
    unnamed x25, local copies, waits for them, and re-layouts  13.3 us
  transfers between devices with their start and end apart: 5, of which 1 were waited for; matrix products, arithmetic and copies ran while one was open for 28% of the time, Pallas kernels for 44%

profile of v1, /device:TPU:7, one launch (start us, length us, event | category | flops | bytes accessed | tf_op | source)
XLA Modules:
  0.0 324.5 jit_solution(2923486803043081081)
XLA Ops:
  0.6 1.1 fusion.61
  1.8 1.3 collective-permute-start
  3.1 5.5 %collective-permute-start.1 = (bf16[1,3,256,192]{2,3,1,0:T(8,128)(2,1)S(1)}, bf16[1,3,256,192]{2,3,1,0:T(8,128)(2,1)S(1)}, u32[]{:S(2)}, u32[]{:S(2)}) collective-permute-start(bf16[1,3,256,192]{2,3,1,0:T(8,128)(2,1)S(1)} %get-tuple-element.19), channel_id=1, source_target_pairs={{128,0},{129,1},{130,2},{131,3},{132,4},{133,5},{134,6},{135,7},{1... | collective-permute-start | bytes 884744 | tf_op jit(solution)/shard_map/ppermute | solution.py:21
  8.6 0.8 copy.63
  9.4 0.7 broadcast_multiply_fusion.1
  10.1 0.1 reshape.297
  10.1 0.1 fusion.27
  10.2 0.1 reduce_window_sum.11
  10.3 0.2 select_reduce_fusion
  10.5 0.6 iota_reduce_fusion
  11.1 0.1 fusion.28
  11.2 0.1 copy.70
  11.3 0.1 mul.713
  11.4 3.5 %reshape.299 = bf16[16,2,128,192]{2,1,3,0:T(2,128)(2,1)} reshape(bf16[1,16,256,192]{2,3,1,0:T(8,128)(2,1)} %param.10) | data formatting | bytes 3145728 | tf_op jit(solution)/shard_map/reshape | solution.py:240
  14.9 1.8 copy.65
  16.6 0.1 broadcast_in_dim.17
  16.7 2.3 gather_fusion.1
  19.1 3.3 %broadcast_select_fusion = bf16[16,3,192,128]{3,2,1,0:T(8,128)(2,1)} fusion(bf16[16,3,192,128]{3,2,1,0:T(8,128)(2,1)} %bitcast.125, pred[16,3]{1,0:T(8,128)(4,1)S(1)} %broadcast_in_dim.17), kind=kLoop, calls=%fused_computation.40 | loop fusion | flops 1179648 | bytes 4718640 | tf_op jit(solution)/shard_map/jit(_where)/select_n | solution.py:255
  22.4 5.6 %all-to-all-start.1 = ((bf16[16,3,192,128]{3,2,1,0:T(8,128)(2,1)}), bf16[16,3,192,128]{3,2,1,0:T(8,128)(2,1)}, u32[]{:S(2)}, u32[]{:S(2)}) async-start(bf16[16,3,192,128]{3,2,1,0:T(8,128)(2,1)} %broadcast_select_fusion), calls=%async_computation.1 | async-start | bytes 4718592 | tf_op jit(solution)/shard_map/all_to_all | solution.py:260
  28.1 0.7 constant_dynamic-update-slice_fusion
  28.7 2.2 fusion.25
  31.0 26.9 %fusion.60 = (f32[16,256]{1,0:T(8,128)S(1)}, f32[1,16,256,192]{2,3,1,0:T(8,128)S(1)}) fusion(f32[192]{0:T(256)S(1)} %bitcast.166, bf16[1,22,262,192]{2,3,1,0:T(8,128)(2,1)S(1)} %fusion.25, f32[192]{0:T(256)S(1)} %bitcast.167, f32[192]{0:T(256)S(1)} %bitcast.139, f32[192]{0:T(256)S(1)} %bitcast.140, ...), kind=kLoop, calls=%fused_computation.91 | loop fusion | flops 115601408 | bytes 80270080 | tf_op jit(solution)/shard_map/reduce_sum | solution.py:208
  58.0 0.3 multiply_reduce_fusion
  58.3 0.3 copy-done.5
  58.6 0.5 fusion.66
  59.2 0.2 copy.75
  59.4 2.1 copy.74
  61.4 32.6 %fusion.65 = (f32[4096,192]{0,1:T(8,128)}, bf16[4096,192]{0,1:T(8,128)(2,1)}) fusion(f32[4096,192]{0,1:T(8,128)} %bitcast.135, bf16[768,192]{0,1:T(8,128)(2,1)S(1)} %copy-done, bf16[4096,192]{0,1:T(8,128)(2,1)S(1)} %bitcast.137, bf16[192,768]{1,0:T(8,128)(2,1)S(1)} %copy-done.6), kind=kOutput, calls=%fused_computation.96 | convolution fusion | flops 2622750720 | bytes 10027008 | tf_op jit(solution)/shard_map/dot_general | solution.py:215
  94.0 2.8 reshape_reshape.3
  96.8 0.6 copy.62
  97.5 2.3 gather_fusion
  99.8 3.8 %all-to-all-start = ((bf16[16,3,192,128]{3,2,1,0:T(8,128)(2,1)}), bf16[16,3,192,128]{3,2,1,0:T(8,128)(2,1)S(1)}, u32[]{:S(2)}, u32[]{:S(2)}) async-start(bf16[16,3,192,128]{3,2,1,0:T(8,128)(2,1)} %bitcast.123), calls=%async_computation | async-start | bytes 4718592 | tf_op jit(solution)/shard_map/all_to_all | solution.py:259
  103.6 3.3 %copy.66 = bf16[8,2,3,192,128]{4,3,2,1,0:T(8,128)(2,1)} copy(bf16[8,2,3,192,128]{4,3,2,0,1:T(8,128)(2,1)} %bitcast.59) | data formatting | bytes 4718592 | tf_op jit(solution)/shard_map/all_to_all | solution.py:260
  106.9 22.0 %all-to-all-done = bf16[16,3,192,128]{3,2,1,0:T(8,128)(2,1)S(1)} async-done(((bf16[16,3,192,128]{3,2,1,0:T(8,128)(2,1)}), bf16[16,3,192,128]{3,2,1,0:T(8,128)(2,1)S(1)}, u32[]{:S(2)}, u32[]{:S(2)}) %all-to-all-start) | async-done | bytes 2359328 | tf_op jit(solution)/shard_map/all_to_all | solution.py:259
  128.9 0.2 copy.64
  129.1 17.3 %shard_map.112 = (bf16[8,6,192,128]{3,2,1,0:T(8,128)(2,1)S(1)}, f32[8,2,6,192,128]{4,3,2,1,0:T(8,128)}) custom-call(bf16[8,6,192,128]{3,2,1,0:T(8,128)(2,1)S(1)} %bitcast.117, bf16[8,6,192,128]{3,2,1,0:T(8,128)(2,1)} %bitcast.126, bf16[8,192,768]{2,1,0:T(8,128)(2,1)} %win_ref.1, bf16[8,192,768]{2,1,0:T(8,128)(2,1)} %bitcast.136), custom_call_target="tpu_custom_call" | custom-call | tf_op jit(solution)/shard_map/pallas_call | solution.py:172
  146.4 1.6 copy.67
  148.0 6.3 %all-to-all-start.2 = ((bf16[8,6,192,128]{3,2,0,1:T(8,128)(2,1)}), bf16[8,6,192,128]{3,2,0,1:T(8,128)(2,1)}, u32[]{:S(2)}, u32[]{:S(2)}) async-start(bf16[8,6,192,128]{3,2,0,1:T(8,128)(2,1)} %copy.67), calls=%async_computation.2 | async-start | bytes 4718592 | tf_op jit(solution)/shard_map/all_to_all | solution.py:264
  154.3 2.9 copy.76
  157.2 142.8 %shard_map.113 = (f32[8,192,768]{2,1,0:T(8,128)}, f32[8,192,768]{2,1,0:T(8,128)}) custom-call(f32[18432,128]{1,0:T(8,128)} %bitcast.122), custom_call_target="tpu_custom_call" | custom-call | tf_op jit(solution)/shard_map/pallas_call | solution.py:132
  300.0 1.8 copy.69
  301.8 1.9 gather_fusion.2
  303.7 1.8 convert_bitcast_fusion
  305.5 2.4 copy.71
  307.9 3.6 %reshape.305 = f32[1,16,256,192]{2,3,1,0:T(8,128)} reshape(f32[16,2,128,192]{2,1,3,0:T(2,128)S(1)} %copy.71) | data formatting | bytes 6291456 | tf_op jit(solution)/shard_map/convert_element_type | solution.py:270
  311.6 5.9 %fusion.26 = bf16[1,16,256,192]{2,3,1,0:T(8,128)(2,1)} fusion(f32[1,16,256,192]{2,3,1,0:T(8,128)} %reshape.305, f32[1,16,256,192]{2,1,3,0:T(8,128)} %bitcast.119), kind=kLoop, calls=%fused_computation.36 | loop fusion | flops 1572864 | bytes 7864320 | tf_op jit(solution)/shard_map/convert_element_type | solution.py:271
  317.4 4.9 %copy.86 = f32[8,192,768]{2,1,0:T(8,128)} copy(f32[8,192,768]{2,1,0:T(8,128)} %get-tuple-element.77) | data formatting | bytes 9437184
  322.3 2.2 copy.87
  (33 shorter events, 0.2 us)
Async XLA Ops:
  0.6 60.8 %copy-start = (bf16[768,192]{0,1:T(8,128)(2,1)S(1)}, bf16[768,192]{0,1:T(8,128)(2,1)}, u32[]{:S(2)}) copy-start(bf16[768,192]{0,1:T(8,128)(2,1)} %param.15) | copy-start | bytes 884740
  1.8 26.2 %collective-permute-start = (bf16[1,3,256,192]{2,3,1,0:T(8,128)(2,1)S(1)}, bf16[1,3,256,192]{2,3,1,0:T(8,128)(2,1)S(1)}, u32[]{:S(2)}, u32[]{:S(2)}) collective-permute-start(bf16[1,3,256,192]{2,3,1,0:T(8,128)(2,1)S(1)} %get-tuple-element.18), channel_id=1, source_target_pairs={{0,128},{1,129},{2,130},{3,131},{4,132},{5,133},{6,134},{7,135},{8... | collective-permute-start | bytes 884744 | tf_op jit(solution)/shard_map/ppermute | solution.py:18
  3.1 25.7 %collective-permute-start.1 = (bf16[1,3,256,192]{2,3,1,0:T(8,128)(2,1)S(1)}, bf16[1,3,256,192]{2,3,1,0:T(8,128)(2,1)S(1)}, u32[]{:S(2)}, u32[]{:S(2)}) collective-permute-start(bf16[1,3,256,192]{2,3,1,0:T(8,128)(2,1)S(1)} %get-tuple-element.19), channel_id=1, source_target_pairs={{128,0},{129,1},{130,2},{131,3},{132,4},{133,5},{134,6},{135,7},{1... | collective-permute-start | bytes 884744 | tf_op jit(solution)/shard_map/ppermute | solution.py:21
  22.4 5.6 %copy-start.4 = (f32[7,7,192]{2,1,0:T(8,128)S(1)}, f32[7,7,192]{2,1,0:T(8,128)}, u32[]{:S(2)}) copy-start(f32[7,7,192]{2,1,0:T(8,128)} %param.12) | copy-start | bytes 112900
  22.4 5.7 %copy-start.2 = (bf16[1,16,256,192]{2,3,1,0:T(8,128)(2,1)S(1)}, bf16[1,16,256,192]{2,3,1,0:T(8,128)(2,1)}, u32[]{:S(2)}) copy-start(bf16[1,16,256,192]{2,3,1,0:T(8,128)(2,1)} %param.9) | copy-start | bytes 4718596
  22.4 77.4 %all-to-all-start.1 = ((bf16[16,3,192,128]{3,2,1,0:T(8,128)(2,1)}), bf16[16,3,192,128]{3,2,1,0:T(8,128)(2,1)}, u32[]{:S(2)}, u32[]{:S(2)}) async-start(bf16[16,3,192,128]{3,2,1,0:T(8,128)(2,1)} %broadcast_select_fusion), calls=%async_computation.1 | async-start | bytes 4718592 | tf_op jit(solution)/shard_map/all_to_all | solution.py:260
  57.9 0.7 copy-start.5
  59.4 2.1 copy-start.6
  99.8 29.1 %all-to-all-start = ((bf16[16,3,192,128]{3,2,1,0:T(8,128)(2,1)}), bf16[16,3,192,128]{3,2,1,0:T(8,128)(2,1)S(1)}, u32[]{:S(2)}, u32[]{:S(2)}) async-start(bf16[16,3,192,128]{3,2,1,0:T(8,128)(2,1)} %bitcast.123), calls=%async_computation | async-start | bytes 4718592 | tf_op jit(solution)/shard_map/all_to_all | solution.py:259
  148.0 6.3 %copy-start.3 = (f32[4096,192]{0,1:T(8,128)S(1)}, f32[4096,192]{0,1:T(8,128)}, u32[]{:S(2)}) copy-start(f32[4096,192]{0,1:T(8,128)} %get-tuple-element.69) | copy-start | bytes 9437188
  148.0 152.0 %all-to-all-start.2 = ((bf16[8,6,192,128]{3,2,0,1:T(8,128)(2,1)}), bf16[8,6,192,128]{3,2,0,1:T(8,128)(2,1)}, u32[]{:S(2)}, u32[]{:S(2)}) async-start(bf16[8,6,192,128]{3,2,0,1:T(8,128)(2,1)} %copy.67), calls=%async_computation.2 | async-start | bytes 4718592 | tf_op jit(solution)/shard_map/all_to_all | solution.py:264
  311.6 10.8 %slice-start = ((s8[4718592]{0:T(1024)(128)(4,1)}), s8[4194304]{0:T(1024)(128)(4,1)S(1)}, s32[]{:S(2)}) async-start(s8[4718592]{0:T(1024)(128)(4,1)} %bitcast.131), calls=%async_computation.3 | async-start | bytes 8388608
  317.4 4.9 %slice-start.1 = ((s8[4718592]{0:T(1024)(128)(4,1)}), s8[524288]{0:T(1024)(128)(4,1)S(1)}, s32[]{:S(2)}) async-start(s8[4718592]{0:T(1024)(128)(4,1)} %bitcast.131), calls=%async_computation.4 | async-start | bytes 1048576
  317.4 7.1 %copy-start.1 = (bf16[768,192]{0,1:T(8,128)(2,1)S(1)}, bf16[768,192]{0,1:T(8,128)(2,1)}, u32[]{:S(2)}) copy-start(bf16[768,192]{0,1:T(8,128)(2,1)} %param.15) | copy-start | bytes 884740

commit v2 on v1

--- a/solution.py
+++ b/solution.py
@@ -32,18 +32,11 @@
     return plan
 
 
-def allreduce_kernel(plan, rows, in_ref, out_in, out_outt, *scratch):
-    stages = len(plan)
-    bufs = scratch[:stages]
-    sums = scratch[stages:2 * stages]
-    staged = scratch[2 * stages:3 * stages]
-    gathered = scratch[3 * stages]
-    rs_send, rs_recv, ag_send, ag_recv = scratch[3 * stages + 1:]
+def plan_bits(plan):
     lat = lax.axis_index("lat")
     dp = lax.axis_index("dp")
     ex = lax.axis_index("exp")
     core = dp % 2
-
     bits, partners = [], []
     for axis, b0, b1 in plan:
         me = dp if axis == "dp" else lat
@@ -52,21 +45,27 @@
         other = me + (1 - 2 * bit) * step
         bits.append(bit)
         partners.append((lat, other, ex) if axis == "dp" else (other, dp, ex))
-
     barrier = pltpu.get_barrier_semaphore()
     for dev in partners:
         pl.semaphore_signal(barrier, 1, device_id=dev, device_id_type=pl.DeviceIdType.MESH)
-    pl.semaphore_wait(barrier, stages)
-
-    def chunked(count, body):
-        chunk = min(count, 1152)
-        lax.fori_loop(0, count // chunk, lambda i, c: (body(pl.multiple_of(i * chunk, 16), chunk), c)[1], 0)
-
-    los = []
-    lo = jnp.int32(0)
+    pl.semaphore_wait(barrier, len(plan))
+    return bits, partners
+
+
+def chunked(count, body):
+    chunk = min(count, 1152)
+    lax.fori_loop(0, count // chunk, lambda i, c: (body(pl.multiple_of(i * chunk, 16), chunk), c)[1], 0)
+
+
+def scatter_kernel(plan, rows, in_ref, seg_ref, *scratch):
+    stages = len(plan)
+    bufs = scratch[:stages]
+    sums = scratch[stages:2 * stages]
+    staged = scratch[2 * stages:3 * stages]
+    rs_send, rs_recv = scratch[3 * stages:]
+    bits, partners = plan_bits(plan)
     for k in range(stages):
         half = rows >> (k + 1)
-        los.append(lo)
         src = in_ref if k == 0 else sums[k - 1]
         keep = bits[k] * half
         give = (1 - bits[k]) * half
@@ -92,16 +91,23 @@
             ].astype(jnp.float32)
 
         chunked(half, add)
-        lo = lo + bits[k] * half
-
-    last = rows >> stages
-    lo = pl.multiple_of(lo, 16)
-    gathered[pl.ds(lo, last)] = sums[stages - 1][...].astype(jnp.bfloat16)
+    seg_ref[...] = sums[stages - 1][...]
+
+
+def gather_kernel(plan, rows, seg_ref, after_ref, out_in, out_outt, gathered, ag_send, ag_recv):
+    stages = len(plan)
+    bits, partners = plan_bits(plan)
+    los = [jnp.int32(0)]
+    for k in range(stages):
+        los.append(los[-1] + bits[k] * (rows >> (k + 1)))
+    lo = pl.multiple_of(los[stages], 16)
+    gathered[pl.ds(lo, rows >> stages)] = seg_ref[...].astype(jnp.bfloat16)
     for k in reversed(range(stages)):
         half = rows >> (k + 1)
+        at = pl.multiple_of(los[k + 1], 16)
         copy = pltpu.make_async_remote_copy(
-            src_ref=gathered.at[pl.ds(pl.multiple_of(lo, 16), half)],
-            dst_ref=gathered.at[pl.ds(pl.multiple_of(lo, 16), half)],
+            src_ref=gathered.at[pl.ds(at, half)],
+            dst_ref=gathered.at[pl.ds(at, half)],
             send_sem=ag_send.at[k],
             recv_sem=ag_recv.at[k],
             device_id=partners[k],
@@ -109,8 +115,6 @@
         )
         copy.start()
         copy.wait()
-        lo = los[k]
-
     experts, channels, hidden = out_in.shape
     pieces = hidden // 128
     for e in range(experts):
@@ -120,25 +124,39 @@
                 dst[e, :, c * 128:(c + 1) * 128] = gathered[at:at + channels].astype(jnp.float32)
 
 
-def tree_allreduce(flat, experts, channels, hidden):
+def reduce_scatter(flat):
     rows = flat.shape[0]
     plan = reduce_plan(lax.axis_size("lat"), lax.axis_size("dp"))
     stages = len(plan)
     scratch = [pltpu.VMEM((rows >> (k + 1), 128), jnp.bfloat16) for k in range(stages)]
     scratch += [pltpu.VMEM((rows >> (k + 1), 128), jnp.float32) for k in range(stages)]
     scratch += [pltpu.VMEM((rows >> (k + 1), 128), jnp.bfloat16) for k in range(stages)]
-    scratch += [pltpu.VMEM((rows, 128), jnp.bfloat16)]
-    scratch += [pltpu.SemaphoreType.DMA((stages,))] * 4
+    scratch += [pltpu.SemaphoreType.DMA((stages,))] * 2
     return pl.pallas_call(
-        lambda *refs: allreduce_kernel(plan, rows, *refs),
-        out_shape=[jax.ShapeDtypeStruct((experts, channels, hidden), jnp.float32)] * 2,
+        lambda *refs: scatter_kernel(plan, rows, *refs),
+        out_shape=jax.ShapeDtypeStruct((rows >> stages, 128), jnp.float32),
         in_specs=[pl.BlockSpec(memory_space=pltpu.VMEM)],
-        out_specs=[pl.BlockSpec(memory_space=pltpu.VMEM)] * 2,
+        out_specs=pl.BlockSpec(memory_space=pltpu.VMEM),
         scratch_shapes=scratch,
         compiler_params=pltpu.CompilerParams(
             collective_id=0, has_side_effects=True, vmem_limit_bytes=62 * 1024 * 1024
         ),
     )(flat)
+
+
+def all_gather(seg, after, rows, experts, channels, hidden):
+    plan = reduce_plan(lax.axis_size("lat"), lax.axis_size("dp"))
+    stages = len(plan)
+    return pl.pallas_call(
+        lambda *refs: gather_kernel(plan, rows, *refs),
+        out_shape=[jax.ShapeDtypeStruct((experts, channels, hidden), jnp.float32)] * 2,
+        in_specs=[pl.BlockSpec(memory_space=pltpu.VMEM), pl.BlockSpec(memory_space=pl.ANY)],
+        out_specs=[pl.BlockSpec(memory_space=pltpu.VMEM)] * 2,
+        scratch_shapes=[pltpu.VMEM((rows, 128), jnp.bfloat16)] + [pltpu.SemaphoreType.DMA((stages,))] * 2,
+        compiler_params=pltpu.CompilerParams(
+            collective_id=1, has_side_effects=True, vmem_limit_bytes=62 * 1024 * 1024
+        ),
+    )(seg, after)
 
 def expert_kernel(x_ref, g_ref, win_ref, wout_ref, out_ref, flat_ref):
     slots = x_ref.shape[0]
@@ -262,13 +280,15 @@
     local = arrived.shape[0]
     results, flat = run_experts(arrived, arrived_grads, exp_in, jnp.transpose(exp_out, (0, 2, 1)))
     returned = lax.all_to_all(results, "exp", split_axis=1, concat_axis=0, tiled=True)
-    grad_in, grad_out_t = tree_allreduce(flat.reshape(-1, 128), local, channels, exp_in.shape[2])
-    grad_out = jnp.transpose(grad_out_t, (0, 2, 1))
+    seg = reduce_scatter(flat.reshape(-1, 128))
     expert_blocks = returned.reshape(EXPERTS * CAP, channels, BLOCK)[slot_of]
     expert_out = jnp.transpose(expert_blocks.reshape(rows, per_row, channels, BLOCK), (0, 1, 3, 2))
     output = (
         dense_out.astype(jnp.float32) + expert_out.reshape(dense_out.shape).astype(jnp.float32)
     ).astype(jnp.bfloat16)
+    rows_all = flat.size // 128
+    grad_in, grad_out_t = all_gather(seg, output, rows_all, local, channels, exp_in.shape[2])
+    grad_out = jnp.transpose(grad_out_t, (0, 2, 1))
     return (output, grad_in, grad_out)
 
 

time: 325 us -> 328 us (level)
  Pallas kernels: 160 us -> 164 us
  other arithmetic: 43.4 us -> 39.8 us
    pallas_call x1 -> x2, Pallas kernels: 143 us -> 147 us  [the longest x1 78.8 us: all_gather(): pl.pallas_call(lambda *refs: gather_kernel(plan, rows, *refs), out_shape=...]
    unnamed x25 -> x27, local copies, waits for them, and re-layouts: 13.3 us -> 14.1 us
  transfers between devices with their start and end apart: 5 -> 5, of which waited for: 1 -> 1; matrix products, arithmetic and copies ran while one was open for 28% -> 28% of each run, Pallas kernels for 44% -> 21%
where the time goes in v2:
time: 328 us; the launch traced here: 326 us
  Pallas kernels  164 us (50%)
  local copies, waits for them, and re-layouts  44.5 us (14%)
  other arithmetic  39.8 us (12%)
  matrix products  31.9 us (10%)
  starting transfers between devices  22.4 us (7%)
  waiting for transfers between devices  22 us (7%)
    pallas_call x1, Pallas kernels, all_gather(): pl.pallas_call(lambda *refs: gather_kernel(plan, rows, *refs), out_shape=...  78.8 us
    pallas_call x1, Pallas kernels, reduce_scatter(): pl.pallas_call(lambda *refs: scatter_kernel(plan, rows, *refs), out_shape...  68.4 us
    dot_general x1, matrix products, dense_block(): reduced = jnp.dot(active, w_reduce, preferred_element_type=jnp.float32)  31.9 us
    reduce_sum x1, other arithmetic, dense_block(): channel_mean = jnp.mean(smoothed, axis=-1, keepdims=True)  26.9 us
    all_to_all x1, waiting for transfers between devices, body(): lax.all_to_all(outgoing, 'exp', split_axis=0, concat_axis=1, tiled=True)  22 us
    pallas_call x1, Pallas kernels, run_experts(): pl.pallas_call(expert_kernel, grid=(experts,), out_shape=[jax.ShapeDtypeS...  17.3 us
    unnamed x27, local copies, waits for them, and re-layouts  14.1 us
  transfers between devices with their start and end apart: 5, of which 1 were waited for; matrix products, arithmetic and copies ran while one was open for 28% of the time, Pallas kernels for 21%

profile of v2, /device:TPU:7, one launch (start us, length us, event | category | flops | bytes accessed | tf_op | source)
XLA Modules:
  0.0 326.0 jit_solution(9486305580856301167)
XLA Ops:
  0.6 1.1 fusion.61
  1.8 1.3 collective-permute-start
  3.1 5.5 %collective-permute-start.1 = (bf16[1,3,256,192]{2,3,1,0:T(8,128)(2,1)S(1)}, bf16[1,3,256,192]{2,3,1,0:T(8,128)(2,1)S(1)}, u32[]{:S(2)}, u32[]{:S(2)}) collective-permute-start(bf16[1,3,256,192]{2,3,1,0:T(8,128)(2,1)S(1)} %get-tuple-element.37), channel_id=1, source_target_pairs={{128,0},{129,1},{130,2},{131,3},{132,4},{133,5},{134,6},{135,7},{1... | collective-permute-start | bytes 884744 | tf_op jit(solution)/shard_map/ppermute | solution.py:21
  8.6 0.8 copy.70
  9.4 0.7 broadcast_multiply_fusion.1
  10.1 0.1 reshape.297
  10.1 0.1 fusion.27
  10.3 0.2 select_reduce_fusion
  10.5 0.6 iota_reduce_fusion
  11.1 0.1 fusion.28
  11.2 0.1 copy.77
  11.3 0.1 mul.713
  11.4 3.5 %reshape.299 = bf16[16,2,128,192]{2,1,3,0:T(2,128)(2,1)} reshape(bf16[1,16,256,192]{2,3,1,0:T(8,128)(2,1)} %param.10) | data formatting | bytes 3145728 | tf_op jit(solution)/shard_map/reshape | solution.py:258
  14.9 1.8 copy.72
  16.6 0.1 broadcast_in_dim.17
  16.7 2.3 gather_fusion.1
  19.1 3.3 %broadcast_select_fusion = bf16[16,3,192,128]{3,2,1,0:T(8,128)(2,1)} fusion(bf16[16,3,192,128]{3,2,1,0:T(8,128)(2,1)} %bitcast.123, pred[16,3]{1,0:T(8,128)(4,1)S(1)} %broadcast_in_dim.17), kind=kLoop, calls=%fused_computation.39 | loop fusion | flops 1179648 | bytes 4718640 | tf_op jit(solution)/shard_map/jit(_where)/select_n | solution.py:273
  22.4 5.6 %all-to-all-start.1 = ((bf16[16,3,192,128]{3,2,1,0:T(8,128)(2,1)}), bf16[16,3,192,128]{3,2,1,0:T(8,128)(2,1)}, u32[]{:S(2)}, u32[]{:S(2)}) async-start(bf16[16,3,192,128]{3,2,1,0:T(8,128)(2,1)} %broadcast_select_fusion), calls=%async_computation.1 | async-start | bytes 4718592 | tf_op jit(solution)/shard_map/all_to_all | solution.py:278
  28.1 0.7 constant_dynamic-update-slice_fusion
  28.7 2.2 fusion.26
  31.0 26.9 %fusion.60 = (f32[16,256]{1,0:T(8,128)S(1)}, f32[1,16,256,192]{2,3,1,0:T(8,128)S(1)}) fusion(f32[192]{0:T(256)S(1)} %bitcast.163, bf16[1,22,262,192]{2,3,1,0:T(8,128)(2,1)S(1)} %fusion.26, f32[192]{0:T(256)S(1)} %bitcast.164, f32[192]{0:T(256)S(1)} %bitcast.136, f32[192]{0:T(256)S(1)} %bitcast.137, ...), kind=kLoop, calls=%fused_computation.90 | loop fusion | flops 115601408 | bytes 80270080 | tf_op jit(solution)/shard_map/reduce_sum | solution.py:226
  58.0 0.3 multiply_reduce_fusion
  58.3 0.3 copy-done.6
  58.6 0.5 fusion.65
  59.2 0.2 copy.82
  59.4 2.1 copy.81
  61.4 31.9 %fusion.16 = bf16[4096,192]{0,1:T(8,128)(2,1)} fusion(f32[4096,192]{0,1:T(8,128)} %bitcast.132, bf16[768,192]{0,1:T(8,128)(2,1)S(1)} %copy-done, bf16[4096,192]{0,1:T(8,128)(2,1)S(1)} %bitcast.134, bf16[192,768]{1,0:T(8,128)(2,1)S(1)} %copy-done.7), kind=kOutput, calls=%fused_computation.27 | convolution fusion | flops 2621964288 | bytes 6881280 | tf_op jit(solution)/shard_map/dot_general | solution.py:233
  93.3 2.8 reshape_reshape.3
  96.2 0.6 copy.69
  96.8 2.3 gather_fusion
  99.1 3.8 %all-to-all-start = ((bf16[16,3,192,128]{3,2,1,0:T(8,128)(2,1)}), bf16[16,3,192,128]{3,2,1,0:T(8,128)(2,1)S(1)}, u32[]{:S(2)}, u32[]{:S(2)}) async-start(bf16[16,3,192,128]{3,2,1,0:T(8,128)(2,1)} %bitcast.121), calls=%async_computation | async-start | bytes 4718592 | tf_op jit(solution)/shard_map/all_to_all | solution.py:277
  102.9 3.3 %copy.73 = bf16[8,2,3,192,128]{4,3,2,1,0:T(8,128)(2,1)} copy(bf16[8,2,3,192,128]{4,3,2,0,1:T(8,128)(2,1)} %bitcast.60) | data formatting | bytes 4718592 | tf_op jit(solution)/shard_map/all_to_all | solution.py:278
  106.2 22.0 %all-to-all-done = bf16[16,3,192,128]{3,2,1,0:T(8,128)(2,1)S(1)} async-done(((bf16[16,3,192,128]{3,2,1,0:T(8,128)(2,1)}), bf16[16,3,192,128]{3,2,1,0:T(8,128)(2,1)S(1)}, u32[]{:S(2)}, u32[]{:S(2)}) %all-to-all-start) | async-done | bytes 2359328 | tf_op jit(solution)/shard_map/all_to_all | solution.py:277
  128.2 0.2 copy.71
  128.4 17.3 %shard_map.112 = (bf16[8,6,192,128]{3,2,1,0:T(8,128)(2,1)S(1)}, f32[8,2,6,192,128]{4,3,2,1,0:T(8,128)}) custom-call(bf16[8,6,192,128]{3,2,1,0:T(8,128)(2,1)S(1)} %bitcast.115, bf16[8,6,192,128]{3,2,1,0:T(8,128)(2,1)} %bitcast.124, bf16[8,192,768]{2,1,0:T(8,128)(2,1)} %win_ref.1, bf16[8,192,768]{2,1,0:T(8,128)(2,1)} %bitcast.133), custom_call_target="tpu_custom_call" | custom-call | tf_op jit(solution)/shard_map/pallas_call | solution.py:190
  145.7 1.6 copy.74
  147.3 6.2 %all-to-all-start.2 = ((bf16[8,6,192,128]{3,2,0,1:T(8,128)(2,1)}), bf16[8,6,192,128]{3,2,0,1:T(8,128)(2,1)}, u32[]{:S(2)}, u32[]{:S(2)}) async-start(bf16[8,6,192,128]{3,2,0,1:T(8,128)(2,1)} %copy.74), calls=%async_computation.2 | async-start | bytes 4718592 | tf_op jit(solution)/shard_map/all_to_all | solution.py:282
  153.5 2.9 copy.68
  156.3 68.4 %shard_map.113.refs_0_ = f32[144,128]{1,0:T(8,128)} custom-call(f32[18432,128]{1,0:T(8,128)} %bitcast.120), custom_call_target="tpu_custom_call" | custom-call | tf_op jit(solution)/shard_map/pallas_call | solution.py:135
  224.8 1.8 copy.76
  226.6 1.9 gather_fusion.2
  228.5 3.9 %copy.78 = f32[16,2,192,128]{2,3,1,0:T(8,128)} copy(bf16[16,2,192,128]{3,2,1,0:T(8,128)(2,1)} %bitcast.128) | data formatting | bytes 4718592 | tf_op jit(solution)/shard_map/convert_element_type | solution.py:287
  232.4 4.0 %fusion.19.refs_1_ = bf16[1,16,256,192]{3,2,1,0:T(8,128)(2,1)S(1)} fusion(f32[1,16,256,192]{3,2,1,0:T(8,128)} %bitcast.116, f32[16,2,192,128]{2,3,1,0:T(8,128)} %copy.78), kind=kLoop, calls=%fused_computation.29 | loop fusion | flops 1572864 | bytes 7864320 | tf_op jit(solution)/shard_map/convert_element_type | solution.py:288
  236.4 1.3 copy-done.2
  237.7 2.2 copy.79
  240.0 78.8 %shard_map.114 = (f32[8,192,768]{2,1,0:T(8,128)}, f32[8,192,768]{2,1,0:T(8,128)}) custom-call(f32[144,128]{1,0:T(8,128)} %shard_map.113.refs_0_, bf16[1,16,256,192]{3,2,1,0:T(8,128)(2,1)} %copy-done.2), custom_call_target="tpu_custom_call" | custom-call | tf_op jit(solution)/shard_map/pallas_call | solution.py:150
  318.8 5.0 %copy.89 = f32[8,192,768]{2,1,0:T(8,128)} copy(f32[8,192,768]{2,1,0:T(8,128)} %get-tuple-element.93) | data formatting | bytes 9437184
  323.8 2.2 copy.90
  (35 shorter events, 0.2 us)
Async XLA Ops:
  0.6 60.8 %copy-start = (bf16[768,192]{0,1:T(8,128)(2,1)S(1)}, bf16[768,192]{0,1:T(8,128)(2,1)}, u32[]{:S(2)}) copy-start(bf16[768,192]{0,1:T(8,128)(2,1)} %param.15) | copy-start | bytes 884740
  1.8 26.2 %collective-permute-start = (bf16[1,3,256,192]{2,3,1,0:T(8,128)(2,1)S(1)}, bf16[1,3,256,192]{2,3,1,0:T(8,128)(2,1)S(1)}, u32[]{:S(2)}, u32[]{:S(2)}) collective-permute-start(bf16[1,3,256,192]{2,3,1,0:T(8,128)(2,1)S(1)} %get-tuple-element.36), channel_id=1, source_target_pairs={{0,128},{1,129},{2,130},{3,131},{4,132},{5,133},{6,134},{7,135},{8... | collective-permute-start | bytes 884744 | tf_op jit(solution)/shard_map/ppermute | solution.py:18
  3.1 25.7 %collective-permute-start.1 = (bf16[1,3,256,192]{2,3,1,0:T(8,128)(2,1)S(1)}, bf16[1,3,256,192]{2,3,1,0:T(8,128)(2,1)S(1)}, u32[]{:S(2)}, u32[]{:S(2)}) collective-permute-start(bf16[1,3,256,192]{2,3,1,0:T(8,128)(2,1)S(1)} %get-tuple-element.37), channel_id=1, source_target_pairs={{128,0},{129,1},{130,2},{131,3},{132,4},{133,5},{134,6},{135,7},{1... | collective-permute-start | bytes 884744 | tf_op jit(solution)/shard_map/ppermute | solution.py:21
  22.4 5.6 %copy-start.5 = (f32[7,7,192]{2,1,0:T(8,128)S(1)}, f32[7,7,192]{2,1,0:T(8,128)}, u32[]{:S(2)}) copy-start(f32[7,7,192]{2,1,0:T(8,128)} %param.12) | copy-start | bytes 112900
  22.4 5.7 %copy-start.3 = (bf16[1,16,256,192]{2,3,1,0:T(8,128)(2,1)S(1)}, bf16[1,16,256,192]{2,3,1,0:T(8,128)(2,1)}, u32[]{:S(2)}) copy-start(bf16[1,16,256,192]{2,3,1,0:T(8,128)(2,1)} %param.9) | copy-start | bytes 4718596
  22.4 76.7 %all-to-all-start.1 = ((bf16[16,3,192,128]{3,2,1,0:T(8,128)(2,1)}), bf16[16,3,192,128]{3,2,1,0:T(8,128)(2,1)}, u32[]{:S(2)}, u32[]{:S(2)}) async-start(bf16[16,3,192,128]{3,2,1,0:T(8,128)(2,1)} %broadcast_select_fusion), calls=%async_computation.1 | async-start | bytes 4718592 | tf_op jit(solution)/shard_map/all_to_all | solution.py:278
  58.0 0.7 copy-start.6
  59.4 2.1 copy-start.7
  99.1 29.1 %all-to-all-start = ((bf16[16,3,192,128]{3,2,1,0:T(8,128)(2,1)}), bf16[16,3,192,128]{3,2,1,0:T(8,128)(2,1)S(1)}, u32[]{:S(2)}, u32[]{:S(2)}) async-start(bf16[16,3,192,128]{3,2,1,0:T(8,128)(2,1)} %bitcast.121), calls=%async_computation | async-start | bytes 4718592 | tf_op jit(solution)/shard_map/all_to_all | solution.py:277
  147.3 6.2 %copy-start.4 = (bf16[4096,192]{0,1:T(8,128)(2,1)S(1)}, bf16[4096,192]{0,1:T(8,128)(2,1)}, u32[]{:S(2)}) copy-start(bf16[4096,192]{0,1:T(8,128)(2,1)} %fusion.16) | copy-start | bytes 4718596
  147.3 77.5 %all-to-all-start.2 = ((bf16[8,6,192,128]{3,2,0,1:T(8,128)(2,1)}), bf16[8,6,192,128]{3,2,0,1:T(8,128)(2,1)}, u32[]{:S(2)}, u32[]{:S(2)}) async-start(bf16[8,6,192,128]{3,2,0,1:T(8,128)(2,1)} %copy.74), calls=%async_computation.2 | async-start | bytes 4718592 | tf_op jit(solution)/shard_map/all_to_all | solution.py:282
  236.4 1.3 copy-start.2
  318.8 5.0 %slice-start = ((s8[4718592]{0:T(1024)(128)(4,1)}), s8[4194304]{0:T(1024)(128)(4,1)S(1)}, s32[]{:S(2)}) async-start(s8[4718592]{0:T(1024)(128)(4,1)} %bitcast.129), calls=%async_computation.3 | async-start | bytes 8388608
  318.8 5.0 %slice-start.1 = ((s8[4718592]{0:T(1024)(128)(4,1)}), s8[524288]{0:T(1024)(128)(4,1)S(1)}, s32[]{:S(2)}) async-start(s8[4718592]{0:T(1024)(128)(4,1)} %bitcast.129), calls=%async_computation.4 | async-start | bytes 1048576
  318.8 7.2 %copy-start.1 = (bf16[768,192]{0,1:T(8,128)(2,1)S(1)}, bf16[768,192]{0,1:T(8,128)(2,1)}, u32[]{:S(2)}) copy-start(bf16[768,192]{0,1:T(8,128)(2,1)} %param.15) | copy-start | bytes 884740

commit v3 on v1

--- a/solution.py
+++ b/solution.py
@@ -74,24 +74,45 @@
         def narrow(at, chunk, src=src, give=give, k=k):
             staged[k][pl.ds(at, chunk)] = src[pl.ds(pl.multiple_of(give + at, 16), chunk)].astype(jnp.bfloat16)
 
-        chunked(half, narrow)
-        copy = pltpu.make_async_remote_copy(
-            src_ref=staged[k],
-            dst_ref=bufs[k],
-            send_sem=rs_send.at[k],
-            recv_sem=rs_recv.at[k],
-            device_id=partners[k],
-            device_id_type=pl.DeviceIdType.MESH,
-        )
-        copy.start()
-        copy.wait()
-
         def add(at, chunk, src=src, keep=keep, k=k):
             sums[k][pl.ds(at, chunk)] = src[pl.ds(pl.multiple_of(keep + at, 16), chunk)] + bufs[k][
                 pl.ds(at, chunk)
             ].astype(jnp.float32)
 
-        chunked(half, add)
+        parts = 2 if half >= 576 else 1
+        piece = half // parts
+        copies = []
+        for p in range(parts):
+            lax.fori_loop(
+                0,
+                piece // min(piece, 1152),
+                lambda i, c, p=p, narrow=narrow: (
+                    narrow(pl.multiple_of(p * piece + i * min(piece, 1152), 16), min(piece, 1152)),
+                    c,
+                )[1],
+                0,
+            )
+            copy = pltpu.make_async_remote_copy(
+                src_ref=staged[k].at[pl.ds(p * piece, piece)],
+                dst_ref=bufs[k].at[pl.ds(p * piece, piece)],
+                send_sem=rs_send.at[2 * k + p],
+                recv_sem=rs_recv.at[2 * k + p],
+                device_id=partners[k],
+                device_id_type=pl.DeviceIdType.MESH,
+            )
+            copy.start()
+            copies.append(copy)
+        for p in range(parts):
+            copies[p].wait()
+            lax.fori_loop(
+                0,
+                piece // min(piece, 1152),
+                lambda i, c, p=p, add=add: (
+                    add(pl.multiple_of(p * piece + i * min(piece, 1152), 16), min(piece, 1152)),
+                    c,
+                )[1],
+                0,
+            )
         lo = lo + bits[k] * half
 
     last = rows >> stages
@@ -128,7 +149,7 @@
     scratch += [pltpu.VMEM((rows >> (k + 1), 128), jnp.float32) for k in range(stages)]
     scratch += [pltpu.VMEM((rows >> (k + 1), 128), jnp.bfloat16) for k in range(stages)]
     scratch += [pltpu.VMEM((rows, 128), jnp.bfloat16)]
-    scratch += [pltpu.SemaphoreType.DMA((stages,))] * 4
+    scratch += [pltpu.SemaphoreType.DMA((2 * stages,))] * 2 + [pltpu.SemaphoreType.DMA((stages,))] * 2
     return pl.pallas_call(
         lambda *refs: allreduce_kernel(plan, rows, *refs),
         out_shape=[jax.ShapeDtypeStruct((experts, channels, hidden), jnp.float32)] * 2,

time: 325 us -> 325 us (level)
  no operation moved by 1% of the time
where the time goes in v3:
time: 325 us; the launch traced here: 324 us
  Pallas kernels  159 us (49%)
  other arithmetic  43.4 us (13%)
  local copies, waits for them, and re-layouts  43.1 us (13%)
  matrix products  32.6 us (10%)
  starting transfers between devices  22.5 us (7%)
  waiting for transfers between devices  22 us (7%)
    pallas_call x1, Pallas kernels, tree_allreduce(): pl.pallas_call(lambda *refs: allreduce_kernel(plan, rows, *refs), out_sha...  142 us
    dot_general x1, matrix products, dense_block(): reduced = jnp.dot(active, w_reduce, preferred_element_type=jnp.float32)  32.6 us
    reduce_sum x1, other arithmetic, dense_block(): channel_mean = jnp.mean(smoothed, axis=-1, keepdims=True)  26.9 us
    all_to_all x1, waiting for transfers between devices, body(): lax.all_to_all(outgoing, 'exp', split_axis=0, concat_axis=1, tiled=True)  22 us
    pallas_call x1, Pallas kernels, run_experts(): pl.pallas_call(expert_kernel, grid=(experts,), out_shape=[jax.ShapeDtypeS...  17.3 us
    unnamed x25, local copies, waits for them, and re-layouts  13.3 us
  transfers between devices with their start and end apart: 5, of which 1 were waited for; matrix products, arithmetic and copies ran while one was open for 28% of the time, Pallas kernels for 44%

profile of v3, /device:TPU:7, one launch (start us, length us, event | category | flops | bytes accessed | tf_op | source)
XLA Modules:
  0.0 323.8 jit_solution(5234347861777125865)
XLA Ops:
  0.6 1.1 fusion.61
  1.8 1.3 collective-permute-start
  3.1 5.5 %collective-permute-start.1 = (bf16[1,3,256,192]{2,3,1,0:T(8,128)(2,1)S(1)}, bf16[1,3,256,192]{2,3,1,0:T(8,128)(2,1)S(1)}, u32[]{:S(2)}, u32[]{:S(2)}) collective-permute-start(bf16[1,3,256,192]{2,3,1,0:T(8,128)(2,1)S(1)} %get-tuple-element.19), channel_id=1, source_target_pairs={{128,0},{129,1},{130,2},{131,3},{132,4},{133,5},{134,6},{135,7},{1... | collective-permute-start | bytes 884744 | tf_op jit(solution)/shard_map/ppermute | solution.py:21
  8.6 0.8 copy.63
  9.4 0.7 broadcast_multiply_fusion.1
  10.1 0.1 reshape.297
  10.1 0.1 fusion.27
  10.2 0.1 reduce_window_sum.11
  10.3 0.2 select_reduce_fusion
  10.5 0.6 iota_reduce_fusion
  11.1 0.1 fusion.28
  11.2 0.1 copy.70
  11.3 0.1 mul.713
  11.4 3.5 %reshape.299 = bf16[16,2,128,192]{2,1,3,0:T(2,128)(2,1)} reshape(bf16[1,16,256,192]{2,3,1,0:T(8,128)(2,1)} %param.10) | data formatting | bytes 3145728 | tf_op jit(solution)/shard_map/reshape | solution.py:261
  14.9 1.8 copy.65
  16.6 0.1 broadcast_in_dim.17
  16.7 2.3 gather_fusion.1
  19.1 3.3 %broadcast_select_fusion = bf16[16,3,192,128]{3,2,1,0:T(8,128)(2,1)} fusion(bf16[16,3,192,128]{3,2,1,0:T(8,128)(2,1)} %bitcast.125, pred[16,3]{1,0:T(8,128)(4,1)S(1)} %broadcast_in_dim.17), kind=kLoop, calls=%fused_computation.40 | loop fusion | flops 1179648 | bytes 4718640 | tf_op jit(solution)/shard_map/jit(_where)/select_n | solution.py:276
  22.4 5.6 %all-to-all-start.1 = ((bf16[16,3,192,128]{3,2,1,0:T(8,128)(2,1)}), bf16[16,3,192,128]{3,2,1,0:T(8,128)(2,1)}, u32[]{:S(2)}, u32[]{:S(2)}) async-start(bf16[16,3,192,128]{3,2,1,0:T(8,128)(2,1)} %broadcast_select_fusion), calls=%async_computation.1 | async-start | bytes 4718592 | tf_op jit(solution)/shard_map/all_to_all | solution.py:281
  28.1 0.7 constant_dynamic-update-slice_fusion
  28.7 2.2 fusion.25
  31.0 26.9 %fusion.60 = (f32[16,256]{1,0:T(8,128)S(1)}, f32[1,16,256,192]{2,3,1,0:T(8,128)S(1)}) fusion(f32[192]{0:T(256)S(1)} %bitcast.166, bf16[1,22,262,192]{2,3,1,0:T(8,128)(2,1)S(1)} %fusion.25, f32[192]{0:T(256)S(1)} %bitcast.167, f32[192]{0:T(256)S(1)} %bitcast.139, f32[192]{0:T(256)S(1)} %bitcast.140, ...), kind=kLoop, calls=%fused_computation.91 | loop fusion | flops 115601408 | bytes 80270080 | tf_op jit(solution)/shard_map/reduce_sum | solution.py:229
  58.0 0.3 multiply_reduce_fusion
  58.3 0.3 copy-done.5
  58.6 0.5 fusion.66
  59.2 0.2 copy.75
  59.4 2.1 copy.74
  61.4 32.6 %fusion.65 = (f32[4096,192]{0,1:T(8,128)}, bf16[4096,192]{0,1:T(8,128)(2,1)}) fusion(f32[4096,192]{0,1:T(8,128)} %bitcast.135, bf16[768,192]{0,1:T(8,128)(2,1)S(1)} %copy-done, bf16[4096,192]{0,1:T(8,128)(2,1)S(1)} %bitcast.137, bf16[192,768]{1,0:T(8,128)(2,1)S(1)} %copy-done.6), kind=kOutput, calls=%fused_computation.96 | convolution fusion | flops 2622750720 | bytes 10027008 | tf_op jit(solution)/shard_map/dot_general | solution.py:236
  94.0 2.8 reshape_reshape.3
  96.8 0.6 copy.62
  97.5 2.3 gather_fusion
  99.8 3.8 %all-to-all-start = ((bf16[16,3,192,128]{3,2,1,0:T(8,128)(2,1)}), bf16[16,3,192,128]{3,2,1,0:T(8,128)(2,1)S(1)}, u32[]{:S(2)}, u32[]{:S(2)}) async-start(bf16[16,3,192,128]{3,2,1,0:T(8,128)(2,1)} %bitcast.123), calls=%async_computation | async-start | bytes 4718592 | tf_op jit(solution)/shard_map/all_to_all | solution.py:280
  103.6 3.3 %copy.66 = bf16[8,2,3,192,128]{4,3,2,1,0:T(8,128)(2,1)} copy(bf16[8,2,3,192,128]{4,3,2,0,1:T(8,128)(2,1)} %bitcast.59) | data formatting | bytes 4718592 | tf_op jit(solution)/shard_map/all_to_all | solution.py:281
  106.9 22.0 %all-to-all-done = bf16[16,3,192,128]{3,2,1,0:T(8,128)(2,1)S(1)} async-done(((bf16[16,3,192,128]{3,2,1,0:T(8,128)(2,1)}), bf16[16,3,192,128]{3,2,1,0:T(8,128)(2,1)S(1)}, u32[]{:S(2)}, u32[]{:S(2)}) %all-to-all-start) | async-done | bytes 2359328 | tf_op jit(solution)/shard_map/all_to_all | solution.py:280
  128.9 0.2 copy.64
  129.1 17.3 %shard_map.112 = (bf16[8,6,192,128]{3,2,1,0:T(8,128)(2,1)S(1)}, f32[8,2,6,192,128]{4,3,2,1,0:T(8,128)}) custom-call(bf16[8,6,192,128]{3,2,1,0:T(8,128)(2,1)S(1)} %bitcast.117, bf16[8,6,192,128]{3,2,1,0:T(8,128)(2,1)} %bitcast.126, bf16[8,192,768]{2,1,0:T(8,128)(2,1)} %win_ref.1, bf16[8,192,768]{2,1,0:T(8,128)(2,1)} %bitcast.136), custom_call_target="tpu_custom_call" | custom-call | tf_op jit(solution)/shard_map/pallas_call | solution.py:193
  146.4 1.6 copy.67
  148.0 6.3 %all-to-all-start.2 = ((bf16[8,6,192,128]{3,2,0,1:T(8,128)(2,1)}), bf16[8,6,192,128]{3,2,0,1:T(8,128)(2,1)}, u32[]{:S(2)}, u32[]{:S(2)}) async-start(bf16[8,6,192,128]{3,2,0,1:T(8,128)(2,1)} %copy.67), calls=%async_computation.2 | async-start | bytes 4718592 | tf_op jit(solution)/shard_map/all_to_all | solution.py:285
  154.3 2.9 copy.76
  157.2 142.0 %shard_map.113 = (f32[8,192,768]{2,1,0:T(8,128)}, f32[8,192,768]{2,1,0:T(8,128)}) custom-call(f32[18432,128]{1,0:T(8,128)} %bitcast.122), custom_call_target="tpu_custom_call" | custom-call | tf_op jit(solution)/shard_map/pallas_call | solution.py:153
  299.3 1.8 copy.69
  301.1 1.9 gather_fusion.2
  303.0 1.8 convert_bitcast_fusion
  304.7 2.4 copy.71
  307.2 3.6 %reshape.305 = f32[1,16,256,192]{2,3,1,0:T(8,128)} reshape(f32[16,2,128,192]{2,1,3,0:T(2,128)S(1)} %copy.71) | data formatting | bytes 6291456 | tf_op jit(solution)/shard_map/convert_element_type | solution.py:291
  310.8 5.9 %fusion.26 = bf16[1,16,256,192]{2,3,1,0:T(8,128)(2,1)} fusion(f32[1,16,256,192]{2,3,1,0:T(8,128)} %reshape.305, f32[1,16,256,192]{2,1,3,0:T(8,128)} %bitcast.119), kind=kLoop, calls=%fused_computation.36 | loop fusion | flops 1572864 | bytes 7864320 | tf_op jit(solution)/shard_map/convert_element_type | solution.py:292
  316.7 4.9 %copy.86 = f32[8,192,768]{2,1,0:T(8,128)} copy(f32[8,192,768]{2,1,0:T(8,128)} %get-tuple-element.77) | data formatting | bytes 9437184
  321.6 2.2 copy.87
  (33 shorter events, 0.2 us)
Async XLA Ops:
  0.6 60.8 %copy-start = (bf16[768,192]{0,1:T(8,128)(2,1)S(1)}, bf16[768,192]{0,1:T(8,128)(2,1)}, u32[]{:S(2)}) copy-start(bf16[768,192]{0,1:T(8,128)(2,1)} %param.15) | copy-start | bytes 884740
  1.8 26.2 %collective-permute-start = (bf16[1,3,256,192]{2,3,1,0:T(8,128)(2,1)S(1)}, bf16[1,3,256,192]{2,3,1,0:T(8,128)(2,1)S(1)}, u32[]{:S(2)}, u32[]{:S(2)}) collective-permute-start(bf16[1,3,256,192]{2,3,1,0:T(8,128)(2,1)S(1)} %get-tuple-element.18), channel_id=1, source_target_pairs={{0,128},{1,129},{2,130},{3,131},{4,132},{5,133},{6,134},{7,135},{8... | collective-permute-start | bytes 884744 | tf_op jit(solution)/shard_map/ppermute | solution.py:18
  3.1 25.7 %collective-permute-start.1 = (bf16[1,3,256,192]{2,3,1,0:T(8,128)(2,1)S(1)}, bf16[1,3,256,192]{2,3,1,0:T(8,128)(2,1)S(1)}, u32[]{:S(2)}, u32[]{:S(2)}) collective-permute-start(bf16[1,3,256,192]{2,3,1,0:T(8,128)(2,1)S(1)} %get-tuple-element.19), channel_id=1, source_target_pairs={{128,0},{129,1},{130,2},{131,3},{132,4},{133,5},{134,6},{135,7},{1... | collective-permute-start | bytes 884744 | tf_op jit(solution)/shard_map/ppermute | solution.py:21
  22.4 5.6 %copy-start.4 = (f32[7,7,192]{2,1,0:T(8,128)S(1)}, f32[7,7,192]{2,1,0:T(8,128)}, u32[]{:S(2)}) copy-start(f32[7,7,192]{2,1,0:T(8,128)} %param.12) | copy-start | bytes 112900
  22.4 5.7 %copy-start.2 = (bf16[1,16,256,192]{2,3,1,0:T(8,128)(2,1)S(1)}, bf16[1,16,256,192]{2,3,1,0:T(8,128)(2,1)}, u32[]{:S(2)}) copy-start(bf16[1,16,256,192]{2,3,1,0:T(8,128)(2,1)} %param.9) | copy-start | bytes 4718596
  22.4 77.4 %all-to-all-start.1 = ((bf16[16,3,192,128]{3,2,1,0:T(8,128)(2,1)}), bf16[16,3,192,128]{3,2,1,0:T(8,128)(2,1)}, u32[]{:S(2)}, u32[]{:S(2)}) async-start(bf16[16,3,192,128]{3,2,1,0:T(8,128)(2,1)} %broadcast_select_fusion), calls=%async_computation.1 | async-start | bytes 4718592 | tf_op jit(solution)/shard_map/all_to_all | solution.py:281
  57.9 0.7 copy-start.5
  59.4 2.1 copy-start.6
  99.8 29.1 %all-to-all-start = ((bf16[16,3,192,128]{3,2,1,0:T(8,128)(2,1)}), bf16[16,3,192,128]{3,2,1,0:T(8,128)(2,1)S(1)}, u32[]{:S(2)}, u32[]{:S(2)}) async-start(bf16[16,3,192,128]{3,2,1,0:T(8,128)(2,1)} %bitcast.123), calls=%async_computation | async-start | bytes 4718592 | tf_op jit(solution)/shard_map/all_to_all | solution.py:280
  148.0 6.3 %copy-start.3 = (f32[4096,192]{0,1:T(8,128)S(1)}, f32[4096,192]{0,1:T(8,128)}, u32[]{:S(2)}) copy-start(f32[4096,192]{0,1:T(8,128)} %get-tuple-element.69) | copy-start | bytes 9437188
  148.0 151.2 %all-to-all-start.2 = ((bf16[8,6,192,128]{3,2,0,1:T(8,128)(2,1)}), bf16[8,6,192,128]{3,2,0,1:T(8,128)(2,1)}, u32[]{:S(2)}, u32[]{:S(2)}) async-start(bf16[8,6,192,128]{3,2,0,1:T(8,128)(2,1)} %copy.67), calls=%async_computation.2 | async-start | bytes 4718592 | tf_op jit(solution)/shard_map/all_to_all | solution.py:285
  310.8 10.8 %slice-start = ((s8[4718592]{0:T(1024)(128)(4,1)}), s8[4194304]{0:T(1024)(128)(4,1)S(1)}, s32[]{:S(2)}) async-start(s8[4718592]{0:T(1024)(128)(4,1)} %bitcast.131), calls=%async_computation.3 | async-start | bytes 8388608
  316.7 4.9 %slice-start.1 = ((s8[4718592]{0:T(1024)(128)(4,1)}), s8[524288]{0:T(1024)(128)(4,1)S(1)}, s32[]{:S(2)}) async-start(s8[4718592]{0:T(1024)(128)(4,1)} %bitcast.131), calls=%async_computation.4 | async-start | bytes 1048576
  316.7 7.1 %copy-start.1 = (bf16[768,192]{0,1:T(8,128)(2,1)S(1)}, bf16[768,192]{0,1:T(8,128)(2,1)}, u32[]{:S(2)}) copy-start(bf16[768,192]{0,1:T(8,128)(2,1)} %param.15) | copy-start | bytes 884740

commit v4 on v3

--- a/solution.py
+++ b/solution.py
@@ -161,7 +161,12 @@
         ),
     )(flat)
 
-def expert_kernel(x_ref, g_ref, win_ref, wout_ref, out_ref, flat_ref):
+def expert_kernel(x_ref, g_ref, win_ref, wout_ref, *refs):
+    if len(refs) == 3:
+        prior_ref, out_ref, flat_ref = refs
+    else:
+        prior_ref = None
+        out_ref, flat_ref = refs
     slots = x_ref.shape[0]
     x_t = jnp.concatenate([x_ref[s] for s in range(slots)], axis=1)
     g_t = jnp.concatenate([g_ref[s] for s in range(slots)], axis=1)
@@ -180,16 +185,23 @@
     scaled = (back * slope).astype(jnp.bfloat16)
     grad_in = jnp.dot(x_t, scaled, preferred_element_type=jnp.float32)
     for c in range(grad_in.shape[1] // 128):
-        flat_ref[0, c] = grad_in[:, c * 128:(c + 1) * 128]
-        flat_ref[1, c] = grad_out_t[:, c * 128:(c + 1) * 128]
-
-
-def run_experts(inputs, grads, w_in, w_out_t):
+        gi = grad_in[:, c * 128:(c + 1) * 128]
+        go = grad_out_t[:, c * 128:(c + 1) * 128]
+        if prior_ref is not None:
+            gi = gi + prior_ref[0, c]
+            go = go + prior_ref[1, c]
+        flat_ref[0, c] = gi
+        flat_ref[1, c] = go
+
+
+def run_experts(inputs, grads, w_in, w_out_t, prior=None):
     experts, slots, channels, width = inputs.shape
     hidden = w_in.shape[2]
     pieces = hidden // 128
     tok = pl.BlockSpec((None, slots, channels, width), lambda e: (e, 0, 0, 0))
     weight = pl.BlockSpec((None, channels, hidden), lambda e: (e, 0, 0))
+    grad_spec = pl.BlockSpec((None, 2, pieces, channels, 128), lambda e: (e, 0, 0, 0, 0))
+    operands = (inputs, grads, w_in, w_out_t) + (() if prior is None else (prior,))
     return pl.pallas_call(
         expert_kernel,
         grid=(experts,),
@@ -197,10 +209,11 @@
             jax.ShapeDtypeStruct(inputs.shape, jnp.bfloat16),
             jax.ShapeDtypeStruct((experts, 2, pieces, channels, 128), jnp.float32),
         ],
-        in_specs=[tok, tok, weight, weight],
-        out_specs=[tok, pl.BlockSpec((None, 2, pieces, channels, 128), lambda e: (e, 0, 0, 0, 0))],
+        in_specs=[tok, tok, weight, weight] + ([] if prior is None else [grad_spec]),
+        out_specs=[tok, grad_spec],
+        input_output_aliases={} if prior is None else {4: 1},
         compiler_params=pltpu.CompilerParams(vmem_limit_bytes=48 * 1024 * 1024),
-    )(inputs, grads, w_in, w_out_t)
+    )(*operands)
 
 def gelu_slope(values):
     return (
@@ -281,7 +294,20 @@
         lax.all_to_all(outgoing_grads, "exp", split_axis=0, concat_axis=1, tiled=True),
     )
     local = arrived.shape[0]
-    results, flat = run_experts(arrived, arrived_grads, exp_in, jnp.transpose(exp_out, (0, 2, 1)))
+    me = lax.axis_index("exp")
+    w_out_t = jnp.transpose(exp_out, (0, 2, 1))
+    own = lax.dynamic_slice_in_dim(outgoing, me * local, local, axis=0)
+    own_grads = lax.dynamic_slice_in_dim(outgoing_grads, me * local, local, axis=0)
+    own_results, flat = run_experts(own, own_grads, exp_in, w_out_t)
+    other = 1 - me
+    far = lax.dynamic_slice_in_dim(arrived, other * CAP, CAP, axis=1)
+    far_grads = lax.dynamic_slice_in_dim(arrived_grads, other * CAP, CAP, axis=1)
+    far_results, flat = run_experts(far, far_grads, exp_in, w_out_t, flat)
+    results = jnp.where(
+        me == 0,
+        jnp.concatenate([own_results, far_results], axis=1),
+        jnp.concatenate([far_results, own_results], axis=1),
+    )
     returned = lax.all_to_all(results, "exp", split_axis=1, concat_axis=0, tiled=True)
     grad_in, grad_out_t = tree_allreduce(flat.reshape(-1, 128), local, channels, exp_in.shape[2])
     grad_out = jnp.transpose(grad_out_t, (0, 2, 1))

time: 325 us -> 342 us (1.052); the launches traced: 324 us -> 335 us
  waiting for transfers between devices: 22 us -> 6.99 us
  matrix products: 32.6 us -> 43.1 us
  Pallas kernels: 159 us -> 169 us
  local copies, waits for them, and re-layouts: 43.1 us -> 48.3 us
    all_to_all x1, waiting for transfers between devices: 22 us -> 6.98 us  [body(): lax.all_to_all(outgoing, 'exp', split_axis=0, concat_axis=1, tiled=True)]
    dot_general x1, matrix products: 32.6 us -> 43.1 us  [dense_block(): reduced = jnp.dot(active, w_reduce, preferred_element_type=jnp.float32)]
    pallas_call x1 -> x2, Pallas kernels: 17.3 us -> 26.7 us  [run_experts(): pl.pallas_call(expert_kernel, grid=(experts,), out_shape=[jax.ShapeDtypeS...]
    unnamed x25 -> x31, local copies, waits for them, and re-layouts: 13.3 us -> 13.7 us
  transfers between devices with their start and end apart: 5 -> 5, of which waited for: 1 -> 1; matrix products, arithmetic and copies ran while one was open for 28% -> 31% of each run, Pallas kernels for 44% -> 46%
where the time goes in v4:
time: 342 us; the launch traced here: 335 us
  Pallas kernels  169 us (49%)
  local copies, waits for them, and re-layouts  48.3 us (14%)
  other arithmetic  43.1 us (13%)
  matrix products  43.1 us (13%)
  starting transfers between devices  23.6 us (7%)
  waiting for transfers between devices  6.99 us (2%)
    pallas_call x1, Pallas kernels, tree_allreduce(): pl.pallas_call(lambda *refs: allreduce_kernel(plan, rows, *refs), out_sha...  142 us
    dot_general x1, matrix products, dense_block(): reduced = jnp.dot(active, w_reduce, preferred_element_type=jnp.float32)  43.1 us
    reduce_sum x1, other arithmetic, dense_block(): channel_mean = jnp.mean(smoothed, axis=-1, keepdims=True)  26.9 us
    pallas_call x2, Pallas kernels, run_experts(): pl.pallas_call(expert_kernel, grid=(experts,), out_shape=[jax.ShapeDtypeS...  26.7 us
    unnamed x31, local copies, waits for them, and re-layouts  13.7 us
    all_to_all x1, waiting for transfers between devices, body(): lax.all_to_all(outgoing, 'exp', split_axis=0, concat_axis=1, tiled=True)  6.98 us
  transfers between devices with their start and end apart: 5, of which 1 were waited for; matrix products, arithmetic and copies ran while one was open for 31% of the time, Pallas kernels for 46%

profile of v4, /device:TPU:7, one launch (start us, length us, event | category | flops | bytes accessed | tf_op | source)
XLA Modules:
  0.0 335.3 jit_solution(15295847645928018540)
XLA Ops:
  0.6 1.1 fusion.61
  1.8 1.3 collective-permute-start
  3.1 5.5 %collective-permute-start.1 = (bf16[1,3,256,192]{2,3,1,0:T(8,128)(2,1)S(1)}, bf16[1,3,256,192]{2,3,1,0:T(8,128)(2,1)S(1)}, u32[]{:S(2)}, u32[]{:S(2)}) collective-permute-start(bf16[1,3,256,192]{2,3,1,0:T(8,128)(2,1)S(1)} %get-tuple-element.23), channel_id=1, source_target_pairs={{128,0},{129,1},{130,2},{131,3},{132,4},{133,5},{134,6},{135,7},{1... | collective-permute-start | bytes 884744 | tf_op jit(solution)/shard_map/ppermute | solution.py:21
  8.6 0.8 copy.66
  9.6 0.2 select_reduce_fusion
  9.8 0.6 iota_reduce_fusion
  10.4 0.1 fusion.28
  10.5 3.5 %reshape.299 = bf16[16,2,128,192]{2,1,3,0:T(2,128)(2,1)} reshape(bf16[1,16,256,192]{2,3,1,0:T(8,128)(2,1)} %param.10) | data formatting | bytes 3145728 | tf_op jit(solution)/shard_map/reshape | solution.py:274
  14.0 1.8 copy.67
  15.8 0.1 broadcast_in_dim.17
  15.9 2.3 gather_fusion.1
  18.2 3.3 broadcast_select_fusion
  21.5 5.6 %all-to-all-start.1 = ((bf16[16,3,192,128]{3,2,1,0:T(8,128)(2,1)}), bf16[16,3,192,128]{3,2,1,0:T(8,128)(2,1)}, u32[]{:S(2)}, u32[]{:S(2)}) async-start(bf16[16,3,192,128]{3,2,1,0:T(8,128)(2,1)} %broadcast_select_fusion), calls=%async_computation.1 | async-start | bytes 4718592 | tf_op jit(solution)/shard_map/all_to_all | solution.py:294
  27.2 0.7 constant_dynamic-update-slice_fusion
  27.9 2.2 fusion.25
  30.2 26.9 %fusion.60 = (f32[16,256]{1,0:T(8,128)S(1)}, f32[1,16,256,192]{2,3,1,0:T(8,128)S(1)}) fusion(f32[192]{0:T(256)S(1)} %bitcast.165, bf16[1,22,262,192]{2,3,1,0:T(8,128)(2,1)S(1)} %fusion.25, f32[192]{0:T(256)S(1)} %bitcast.166, f32[192]{0:T(256)S(1)} %bitcast.138, f32[192]{0:T(256)S(1)} %bitcast.139, ...), kind=kLoop, calls=%fused_computation.96 | loop fusion | flops 115601408 | bytes 80270080 | tf_op jit(solution)/shard_map/reduce_sum | solution.py:242
  57.1 0.3 multiply_reduce_fusion
  57.5 0.3 copy-done.8
  57.8 0.5 fusion.66
  58.4 0.2 copy.78
  58.5 2.1 copy.77
  60.6 43.1 %fusion.65 = (f32[4096,192]{0,1:T(8,128)}, bf16[4096,192]{0,1:T(8,128)(2,1)}) fusion(f32[4096,192]{0,1:T(8,128)} %bitcast.135, bf16[768,192]{0,1:T(8,128)(2,1)S(1)} %copy-done, bf16[4096,192]{0,1:T(8,128)(2,1)S(1)} %bitcast.136, bf16[192,768]{1,0:T(8,128)(2,1)S(1)} %copy-done.9), kind=kOutput, calls=%fused_computation.101 | convolution fusion | flops 2622750720 | bytes 10027008 | tf_op jit(solution)/shard_map/dot_general | solution.py:249
  103.7 2.8 reshape_reshape.3
  106.5 0.6 copy.65
  107.2 2.3 gather_fusion
  109.5 4.9 %all-to-all-start = ((bf16[16,3,192,128]{3,2,1,0:T(8,128)(2,1)}), bf16[16,3,192,128]{3,2,1,0:T(8,128)(2,1)}, u32[]{:S(2)}, u32[]{:S(2)}) async-start(bf16[16,3,192,128]{3,2,1,0:T(8,128)(2,1)} %bitcast.51), calls=%async_computation | async-start | bytes 4718592 | tf_op jit(solution)/shard_map/all_to_all | solution.py:293
  114.4 1.5 constant_dynamic-slice_fusion.2.g_ref
  115.9 1.4 constant_dynamic-slice_fusion.3.x_ref
  117.3 12.2 %shard_map.112 = (bf16[8,3,192,128]{3,2,1,0:T(8,128)(2,1)S(1)}, f32[8,2,6,192,128]{4,3,2,1,0:T(8,128)}) custom-call(bf16[8,3,192,128]{3,2,1,0:T(8,128)(2,1)S(1)} %constant_dynamic-slice_fusion.3.x_ref, bf16[8,3,192,128]{3,2,1,0:T(8,128)(2,1)S(1)} %constant_dynamic-slice_fusion.2.g_ref, bf16[8,192,768]{2,1,0:T(8,128)(2,1)S(1)} %copy-done.2, ...), custom_call_target="tpu_custom_call" | custom-call | tf_op jit(solution)/shard_map/pallas_call | solution.py:205
  129.5 3.3 copy.69
  132.8 7.0 %all-to-all-done = bf16[16,3,192,128]{3,2,1,0:T(8,128)(2,1)} async-done(((bf16[16,3,192,128]{3,2,1,0:T(8,128)(2,1)}), bf16[16,3,192,128]{3,2,1,0:T(8,128)(2,1)}, u32[]{:S(2)}, u32[]{:S(2)}) %all-to-all-start) | async-done | bytes 2359328 | tf_op jit(solution)/shard_map/all_to_all | solution.py:293
  139.8 2.0 copy.68
  141.8 0.4 copy-done.4
  142.2 0.2 constant_dynamic-slice_fusion
  142.4 14.5 %shard_map.113 = (bf16[8,3,192,128]{3,2,1,0:T(8,128)(2,1)S(1)}, f32[8,2,6,192,128]{4,3,2,1,0:T(8,128)}) custom-call(bf16[8,3,192,128]{3,2,1,0:T(8,128)(2,1)S(1)} %get-tuple-element.76.x_ref, bf16[8,3,192,128]{3,2,1,0:T(8,128)(2,1)S(1)} %get-tuple-element.75.g_ref, bf16[8,192,768]{2,1,0:T(8,128)(2,1)S(1)} %copy-done.2, ...), custom_call_target="tpu_custom_call", output_to_operand_aliasing={{1}: (4, {})} | custom-call | tf_op jit(solution)/shard_map/pallas_call | solution.py:205
  156.9 0.4 maximum_select_fusion
  157.3 1.7 copy.70
  158.9 6.3 %all-to-all-start.2 = ((bf16[8,6,192,128]{3,2,0,1:T(8,128)(2,1)}), bf16[8,6,192,128]{3,2,0,1:T(8,128)(2,1)}, u32[]{:S(2)}, u32[]{:S(2)}) async-start(bf16[8,6,192,128]{3,2,0,1:T(8,128)(2,1)} %copy.70), calls=%async_computation.2 | async-start | bytes 4718592 | tf_op jit(solution)/shard_map/all_to_all | solution.py:311
  165.5 2.9 copy.79
  168.3 142.0 %shard_map.114 = (f32[8,192,768]{2,1,0:T(8,128)}, f32[8,192,768]{2,1,0:T(8,128)}) custom-call(f32[18432,128]{1,0:T(8,128)} %bitcast.117), custom_call_target="tpu_custom_call" | custom-call | tf_op jit(solution)/shard_map/pallas_call | solution.py:153
  310.4 1.8 copy.72
  312.2 1.9 gather_fusion.2
  314.1 1.8 convert_bitcast_fusion
  315.8 2.4 copy.74
  318.3 3.6 %reshape.305 = f32[1,16,256,192]{2,3,1,0:T(8,128)} reshape(f32[16,2,128,192]{2,1,3,0:T(2,128)S(1)} %copy.74) | data formatting | bytes 6291456 | tf_op jit(solution)/shard_map/convert_element_type | solution.py:317
  321.9 5.9 %fusion.26 = bf16[1,16,256,192]{2,3,1,0:T(8,128)(2,1)} fusion(f32[1,16,256,192]{2,3,1,0:T(8,128)} %reshape.305, f32[1,16,256,192]{2,1,3,0:T(8,128)} %bitcast.119), kind=kLoop, calls=%fused_computation.36 | loop fusion | flops 1572864 | bytes 7864320 | tf_op jit(solution)/shard_map/convert_element_type | solution.py:318
  327.8 4.9 %copy.90 = f32[8,192,768]{2,1,0:T(8,128)} copy(f32[8,192,768]{2,1,0:T(8,128)} %get-tuple-element.81) | data formatting | bytes 9437184
  332.7 2.2 copy.91
  (45 shorter events, 0.6 us)
Async XLA Ops:
  0.6 60.0 %copy-start = (bf16[768,192]{0,1:T(8,128)(2,1)S(1)}, bf16[768,192]{0,1:T(8,128)(2,1)}, u32[]{:S(2)}) copy-start(bf16[768,192]{0,1:T(8,128)(2,1)} %param.15) | copy-start | bytes 884740
  1.8 25.4 %collective-permute-start = (bf16[1,3,256,192]{2,3,1,0:T(8,128)(2,1)S(1)}, bf16[1,3,256,192]{2,3,1,0:T(8,128)(2,1)S(1)}, u32[]{:S(2)}, u32[]{:S(2)}) collective-permute-start(bf16[1,3,256,192]{2,3,1,0:T(8,128)(2,1)S(1)} %get-tuple-element.22), channel_id=1, source_target_pairs={{0,128},{1,129},{2,130},{3,131},{4,132},{5,133},{6,134},{7,135},{8... | collective-permute-start | bytes 884744 | tf_op jit(solution)/shard_map/ppermute | solution.py:18
  3.1 24.8 %collective-permute-start.1 = (bf16[1,3,256,192]{2,3,1,0:T(8,128)(2,1)S(1)}, bf16[1,3,256,192]{2,3,1,0:T(8,128)(2,1)S(1)}, u32[]{:S(2)}, u32[]{:S(2)}) collective-permute-start(bf16[1,3,256,192]{2,3,1,0:T(8,128)(2,1)S(1)} %get-tuple-element.23), channel_id=1, source_target_pairs={{128,0},{129,1},{130,2},{131,3},{132,4},{133,5},{134,6},{135,7},{1... | collective-permute-start | bytes 884744 | tf_op jit(solution)/shard_map/ppermute | solution.py:21
  21.5 5.6 %copy-start.6 = (f32[7,7,192]{2,1,0:T(8,128)S(1)}, f32[7,7,192]{2,1,0:T(8,128)}, u32[]{:S(2)}) copy-start(f32[7,7,192]{2,1,0:T(8,128)} %param.12) | copy-start | bytes 112900
  21.5 5.7 %copy-start.3 = (bf16[1,16,256,192]{2,3,1,0:T(8,128)(2,1)S(1)}, bf16[1,16,256,192]{2,3,1,0:T(8,128)(2,1)}, u32[]{:S(2)}) copy-start(bf16[1,16,256,192]{2,3,1,0:T(8,128)(2,1)} %param.9) | copy-start | bytes 4718596
  21.5 88.0 %all-to-all-start.1 = ((bf16[16,3,192,128]{3,2,1,0:T(8,128)(2,1)}), bf16[16,3,192,128]{3,2,1,0:T(8,128)(2,1)}, u32[]{:S(2)}, u32[]{:S(2)}) async-start(bf16[16,3,192,128]{3,2,1,0:T(8,128)(2,1)} %broadcast_select_fusion), calls=%async_computation.1 | async-start | bytes 4718592 | tf_op jit(solution)/shard_map/all_to_all | solution.py:294
  57.1 0.7 copy-start.8
  58.5 2.1 copy-start.9
  109.5 30.3 %all-to-all-start = ((bf16[16,3,192,128]{3,2,1,0:T(8,128)(2,1)}), bf16[16,3,192,128]{3,2,1,0:T(8,128)(2,1)}, u32[]{:S(2)}, u32[]{:S(2)}) async-start(bf16[16,3,192,128]{3,2,1,0:T(8,128)(2,1)} %bitcast.51), calls=%async_computation | async-start | bytes 4718592 | tf_op jit(solution)/shard_map/all_to_all | solution.py:293
  114.4 2.9 copy-start.2
  139.8 2.4 copy-start.4
  158.9 6.3 %copy-start.7 = (s32[1,16,2,1]{1,3,2,0:T(1,128)S(1)}, s32[1,16,2,1]{1,3,2,0:T(1,128)}, u32[]{:S(2)}) copy-start(s32[1,16,2,1]{1,3,2,0:T(1,128)} %param.11) | copy-start | bytes 388
  158.9 6.5 %copy-start.5 = (f32[4096,192]{0,1:T(8,128)S(1)}, f32[4096,192]{0,1:T(8,128)}, u32[]{:S(2)}) copy-start(f32[4096,192]{0,1:T(8,128)} %get-tuple-element.73) | copy-start | bytes 9437188
  158.9 151.4 %all-to-all-start.2 = ((bf16[8,6,192,128]{3,2,0,1:T(8,128)(2,1)}), bf16[8,6,192,128]{3,2,0,1:T(8,128)(2,1)}, u32[]{:S(2)}, u32[]{:S(2)}) async-start(bf16[8,6,192,128]{3,2,0,1:T(8,128)(2,1)} %copy.70), calls=%async_computation.2 | async-start | bytes 4718592 | tf_op jit(solution)/shard_map/all_to_all | solution.py:311
  321.9 10.8 %slice-start = ((s8[4718592]{0:T(1024)(128)(4,1)}), s8[4194304]{0:T(1024)(128)(4,1)S(1)}, s32[]{:S(2)}) async-start(s8[4718592]{0:T(1024)(128)(4,1)} %bitcast.131), calls=%async_computation.3 | async-start | bytes 8388608
  327.8 4.9 %slice-start.1 = ((s8[4718592]{0:T(1024)(128)(4,1)}), s8[524288]{0:T(1024)(128)(4,1)S(1)}, s32[]{:S(2)}) async-start(s8[4718592]{0:T(1024)(128)(4,1)} %bitcast.131), calls=%async_computation.4 | async-start | bytes 1048576
  327.8 7.1 %copy-start.1 = (bf16[768,192]{0,1:T(8,128)(2,1)S(1)}, bf16[768,192]{0,1:T(8,128)(2,1)}, u32[]{:S(2)}) copy-start(bf16[768,192]{0,1:T(8,128)(2,1)} %param.15) | copy-start | bytes 884740

commit v5 on v3

--- a/solution.py
+++ b/solution.py
@@ -202,6 +202,29 @@
         compiler_params=pltpu.CompilerParams(vmem_limit_bytes=48 * 1024 * 1024),
     )(inputs, grads, w_in, w_out_t)
 
+def assemble_kernel(slot_ref, dense_ref, ret_ref, out_ref):
+    per_row = dense_ref.shape[2] // ret_ref.shape[2]
+    width = ret_ref.shape[2]
+    for b in range(dense_ref.shape[0] * per_row):
+        h, k = b // per_row, b % per_row
+        piece = dense_ref[h, :, k * width:(k + 1) * width].astype(jnp.float32)
+        piece = piece + ret_ref[slot_ref[b]].astype(jnp.float32)
+        out_ref[h, :, k * width:(k + 1) * width] = piece.astype(out_ref.dtype)
+
+
+def assemble(slot_of, dense_t, ret):
+    return pl.pallas_call(
+        assemble_kernel,
+        out_shape=jax.ShapeDtypeStruct(dense_t.shape, dense_t.dtype),
+        in_specs=[
+            pl.BlockSpec(memory_space=pltpu.SMEM),
+            pl.BlockSpec(memory_space=pltpu.VMEM),
+            pl.BlockSpec(memory_space=pltpu.VMEM),
+        ],
+        out_specs=pl.BlockSpec(memory_space=pltpu.VMEM),
+    )(slot_of, dense_t, ret)
+
+
 def gelu_slope(values):
     return (
         0.5 * (1.0 + lax.erf(values * 0.7071067811865476))
@@ -285,11 +308,9 @@
     returned = lax.all_to_all(results, "exp", split_axis=1, concat_axis=0, tiled=True)
     grad_in, grad_out_t = tree_allreduce(flat.reshape(-1, 128), local, channels, exp_in.shape[2])
     grad_out = jnp.transpose(grad_out_t, (0, 2, 1))
-    expert_blocks = returned.reshape(EXPERTS * CAP, channels, BLOCK)[slot_of]
-    expert_out = jnp.transpose(expert_blocks.reshape(rows, per_row, channels, BLOCK), (0, 1, 3, 2))
-    output = (
-        dense_out.astype(jnp.float32) + expert_out.reshape(dense_out.shape).astype(jnp.float32)
-    ).astype(jnp.bfloat16)
+    dense_t = jnp.transpose(dense_out.reshape(rows, width, channels), (0, 2, 1))
+    out_t = assemble(slot_of.astype(jnp.int32), dense_t, returned.reshape(EXPERTS * CAP, channels, BLOCK))
+    output = jnp.transpose(out_t, (0, 2, 1)).reshape(dense_out.shape)
     return (output, grad_in, grad_out)
 
 

time: 325 us -> 311 us (0.957)
  local copies, waits for them, and re-layouts: 43.1 us -> 33.4 us
  other arithmetic: 43.4 us -> 35.9 us
  Pallas kernels: 159 us -> 163 us
    convert_element_type x2 -> x0, other arithmetic: 7.63 us -> none  [the longest x1 5.88 us: body(): output = (dense_out.astype(jnp.float32) + expert_out.reshape(dense_out.sh...]
    convert_element_type x2 -> x0, local copies, waits for them, and re-layouts: 6.08 us -> none  [body(): expert_out.reshape(dense_out.shape).astype(jnp.float32)]
    pallas_call x0 -> x1, Pallas kernels: none -> 3.7 us  [assemble(): pl.pallas_call(assemble_kernel, out_shape=jax.ShapeDtypeStruct(dense_t.sh...]
    unnamed x25 -> x26, local copies, waits for them, and re-layouts: 13.3 us -> 11.5 us
  transfers between devices with their start and end apart: 5 -> 5, of which waited for: 1 -> 1; matrix products, arithmetic and copies ran while one was open for 28% -> 28% of each run, Pallas kernels for 44% -> 46%
where the time goes in v5:
time: 311 us; the launch traced here: 310 us
  Pallas kernels  163 us (52%)
  other arithmetic  35.9 us (12%)
  local copies, waits for them, and re-layouts  33.4 us (11%)
  matrix products  31.5 us (10%)
  starting transfers between devices  23.8 us (8%)
  waiting for transfers between devices  22 us (7%)
    pallas_call x1, Pallas kernels, tree_allreduce(): pl.pallas_call(lambda *refs: allreduce_kernel(plan, rows, *refs), out_sha...  142 us
    dot_general x1, matrix products, dense_block(): reduced = jnp.dot(active, w_reduce, preferred_element_type=jnp.float32)  31.5 us
    reduce_sum x1, other arithmetic, dense_block(): channel_mean = jnp.mean(smoothed, axis=-1, keepdims=True)  26.9 us
    all_to_all x1, waiting for transfers between devices, body(): lax.all_to_all(outgoing, 'exp', split_axis=0, concat_axis=1, tiled=True)  22 us
    pallas_call x1, Pallas kernels, run_experts(): pl.pallas_call(expert_kernel, grid=(experts,), out_shape=[jax.ShapeDtypeS...  17.3 us
    unnamed x26, local copies, waits for them, and re-layouts  11.5 us
    ppermute x1, starting transfers between devices, with_halo(): lax.ppermute(lax.slice_in_dim(block, 0, width, axis=dim), axis, backward)  6.92 us
  transfers between devices with their start and end apart: 5, of which 1 were waited for; matrix products, arithmetic and copies ran while one was open for 28% of the time, Pallas kernels for 46%

profile of v5, /device:TPU:7, one launch (start us, length us, event | category | flops | bytes accessed | tf_op | source)
XLA Modules:
  0.0 310.4 jit_solution(4744283705389254258)
XLA Ops:
  0.6 0.0 copy-start
  0.6 1.9 fusion.59
  2.6 1.3 collective-permute-start
  3.9 6.9 %collective-permute-start.1 = (bf16[1,3,256,192]{2,3,1,0:T(8,128)(2,1)}, bf16[1,3,256,192]{2,3,1,0:T(8,128)(2,1)}, u32[]{:S(2)}, u32[]{:S(2)}) collective-permute-start(bf16[1,3,256,192]{2,3,1,0:T(8,128)(2,1)} %get-tuple-element.19), channel_id=1, source_target_pairs={{128,0},{129,1},{130,2},{131,3},{132,4},{133,5},{134,6},{135,7},{1... | collective-permute-start | bytes 884744 | tf_op jit(solution)/shard_map/ppermute | solution.py:21
  10.8 0.8 copy.42
  11.6 0.1 reshape.224
  11.6 0.1 fusion.27
  11.7 0.1 reduce_window_sum.11
  11.8 0.2 select_reduce_fusion
  12.0 0.6 iota_reduce_fusion
  12.6 0.1 fusion.26
  12.7 2.4 reshape.228
  15.1 0.4 copy.48
  15.4 0.1 broadcast_in_dim.26
  15.5 2.3 gather_fusion.1
  17.9 3.3 %broadcast_select_fusion = bf16[16,3,192,128]{3,2,1,0:T(8,128)(2,1)} fusion(bf16[16,3,192,128]{3,2,1,0:T(8,128)(2,1)} %bitcast.114, pred[16,3]{1,0:T(8,128)(4,1)S(1)} %broadcast_in_dim.26), kind=kLoop, calls=%fused_computation.36 | loop fusion | flops 1179648 | bytes 4718640 | tf_op jit(solution)/shard_map/jit(_where)/select_n | solution.py:299
  21.2 5.6 %all-to-all-start.1 = ((bf16[16,3,192,128]{3,2,1,0:T(8,128)(2,1)}), bf16[16,3,192,128]{3,2,1,0:T(8,128)(2,1)}, u32[]{:S(2)}, u32[]{:S(2)}) async-start(bf16[16,3,192,128]{3,2,1,0:T(8,128)(2,1)} %broadcast_select_fusion), calls=%async_computation.1 | async-start | bytes 4718592 | tf_op jit(solution)/shard_map/all_to_all | solution.py:304
  26.8 0.0 collective-permute-done
  26.8 1.0 constant_dynamic-update-slice_fusion.1
  27.8 0.6 constant_dynamic-update-slice_fusion
  28.5 2.1 copy.53
  30.5 3.2 %fusion.25 = bf16[1,22,262,192]{2,3,1,0:T(8,128)(2,1)S(1)} fusion(bf16[1,3,256,192]{2,3,1,0:T(8,128)(2,1)} %collective-permute-done.1, bf16[1,16,256,192]{2,3,1,0:T(8,128)(2,1)S(1)} %copy-done.2, bf16[1,3,256,192]{2,3,1,0:T(8,128)(2,1)} %collective-permute-done), kind=kLoop, calls=%fused_computation.32 | loop fusion | flops 13280256 | bytes 4376064 | tf_op jit(solution)/shard_map/concatenate | solution.py:22
  33.7 1.0 constant_dynamic-update-slice_fusion.2
  34.7 26.9 %fusion.58 = (f32[16,256]{1,0:T(8,128)S(1)}, f32[1,16,256,192]{2,3,1,0:T(8,128)S(1)}) fusion(f32[192]{0:T(256)S(1)} %bitcast.155, bf16[1,22,262,192]{2,3,1,0:T(8,128)(2,1)S(1)} %fusion.25, f32[192]{0:T(256)S(1)} %bitcast.156, f32[192]{0:T(256)S(1)} %bitcast.128, f32[192]{0:T(256)S(1)} %bitcast.129, ...), kind=kLoop, calls=%fused_computation.83 | loop fusion | flops 115601408 | bytes 80270080 | tf_op jit(solution)/shard_map/reduce_sum | solution.py:252
  61.6 0.0 copy-start.6
  61.7 0.3 multiply_reduce_fusion
  62.0 0.3 copy-done.6
  62.3 0.5 fusion.63
  62.9 0.2 copy.54
  63.0 31.5 %fusion.16 = bf16[4096,192]{0,1:T(8,128)(2,1)S(1)} fusion(f32[4096,192]{0,1:T(8,128)} %bitcast.123, bf16[768,192]{0,1:T(8,128)(2,1)S(1)} %copy-done, bf16[4096,192]{0,1:T(8,128)(2,1)S(1)} %bitcast.125, bf16[192,768]{1,0:T(8,128)(2,1)} %param.14), kind=kOutput, calls=%fused_computation.26 | convolution fusion | flops 2621964288 | bytes 6881280 | tf_op jit(solution)/shard_map/dot_general | solution.py:259
  94.5 0.0 copy-start.3
  94.5 1.1 reshape_reshape.7
  95.7 0.6 copy.46
  96.3 2.3 gather_fusion
  98.6 0.0 all-to-all-done.1
  98.6 3.8 %all-to-all-start = ((bf16[16,3,192,128]{3,2,1,0:T(8,128)(2,1)}), bf16[16,3,192,128]{3,2,1,0:T(8,128)(2,1)S(1)}, u32[]{:S(2)}, u32[]{:S(2)}) async-start(bf16[16,3,192,128]{3,2,1,0:T(8,128)(2,1)} %bitcast.111), calls=%async_computation | async-start | bytes 4718592 | tf_op jit(solution)/shard_map/all_to_all | solution.py:303
  102.5 3.3 %copy.49 = bf16[8,2,3,192,128]{4,3,2,1,0:T(8,128)(2,1)} copy(bf16[8,2,3,192,128]{4,3,2,0,1:T(8,128)(2,1)} %bitcast.60) | data formatting | bytes 4718592 | tf_op jit(solution)/shard_map/all_to_all | solution.py:304
  105.7 22.0 %all-to-all-done = bf16[16,3,192,128]{3,2,1,0:T(8,128)(2,1)S(1)} async-done(((bf16[16,3,192,128]{3,2,1,0:T(8,128)(2,1)}), bf16[16,3,192,128]{3,2,1,0:T(8,128)(2,1)S(1)}, u32[]{:S(2)}, u32[]{:S(2)}) %all-to-all-start) | async-done | bytes 2359328 | tf_op jit(solution)/shard_map/all_to_all | solution.py:303
  127.7 0.2 copy.47
  127.9 17.3 %shard_map.112 = (bf16[8,6,192,128]{3,2,1,0:T(8,128)(2,1)S(1)}, f32[8,2,6,192,128]{4,3,2,1,0:T(8,128)}) custom-call(bf16[8,6,192,128]{3,2,1,0:T(8,128)(2,1)S(1)} %bitcast.106, bf16[8,6,192,128]{3,2,1,0:T(8,128)(2,1)} %bitcast.115, bf16[8,192,768]{2,1,0:T(8,128)(2,1)} %win_ref.1, bf16[8,192,768]{2,1,0:T(8,128)(2,1)} %bitcast.124), custom_call_target="tpu_custom_call" | custom-call | tf_op jit(solution)/shard_map/pallas_call | solution.py:193
  145.2 1.6 copy.50
  146.8 6.2 %all-to-all-start.2 = ((bf16[8,6,192,128]{3,2,0,1:T(8,128)(2,1)}), bf16[8,6,192,128]{3,2,0,1:T(8,128)(2,1)}, u32[]{:S(2)}, u32[]{:S(2)}) async-start(bf16[8,6,192,128]{3,2,0,1:T(8,128)(2,1)} %copy.50), calls=%async_computation.2 | async-start | bytes 4718592 | tf_op jit(solution)/shard_map/all_to_all | solution.py:308
  153.0 1.3 copy.58
  154.3 141.9 %shard_map.114 = (f32[8,192,768]{2,1,0:T(8,128)}, f32[8,192,768]{2,1,0:T(8,128)}) custom-call(f32[18432,128]{1,0:T(8,128)} %bitcast.110), custom_call_target="tpu_custom_call" | custom-call | tf_op jit(solution)/shard_map/pallas_call | solution.py:153
  296.2 3.2 %copy.51 = bf16[8,2,3,192,128]{4,3,2,0,1:T(8,128)(2,1)} copy(bf16[8,2,3,192,128]{4,3,0,2,1:T(8,128)(2,1)} %bitcast.63) | data formatting | bytes 4718592 | tf_op jit(solution)/shard_map/all_to_all | solution.py:308
  299.5 3.7 %shard_map.113 = bf16[16,192,256]{2,1,0:T(8,128)(2,1)} custom-call(s32[32]{0:T(128)} %copy-done.7, bf16[16,192,256]{2,1,0:T(8,128)(2,1)} %bitcast.119, bf16[48,192,128]{2,1,0:T(8,128)(2,1)} %bitcast.113), custom_call_target="tpu_custom_call" | custom-call | tf_op jit(solution)/shard_map/pallas_call | solution.py:216
  303.2 5.0 %copy.63 = f32[8,192,768]{2,1,0:T(8,128)} copy(f32[8,192,768]{2,1,0:T(8,128)} %get-tuple-element.73) | data formatting | bytes 9437184
  308.2 2.2 copy.64
  (27 shorter events, 0.1 us)
Async XLA Ops:
  0.6 62.4 %copy-start = (bf16[768,192]{0,1:T(8,128)(2,1)S(1)}, bf16[768,192]{0,1:T(8,128)(2,1)}, u32[]{:S(2)}) copy-start(bf16[768,192]{0,1:T(8,128)(2,1)} %param.15) | copy-start | bytes 884740
  2.6 24.2 %collective-permute-start = (bf16[1,3,256,192]{2,3,1,0:T(8,128)(2,1)}, bf16[1,3,256,192]{2,3,1,0:T(8,128)(2,1)}, u32[]{:S(2)}, u32[]{:S(2)}) collective-permute-start(bf16[1,3,256,192]{2,3,1,0:T(8,128)(2,1)} %get-tuple-element.18), channel_id=1, source_target_pairs={{0,128},{1,129},{2,130},{3,131},{4,132},{5,133},{6,134},{7,135},{8... | collective-permute-start | bytes 884744 | tf_op jit(solution)/shard_map/ppermute | solution.py:18
  3.9 26.6 %collective-permute-start.1 = (bf16[1,3,256,192]{2,3,1,0:T(8,128)(2,1)}, bf16[1,3,256,192]{2,3,1,0:T(8,128)(2,1)}, u32[]{:S(2)}, u32[]{:S(2)}) collective-permute-start(bf16[1,3,256,192]{2,3,1,0:T(8,128)(2,1)} %get-tuple-element.19), channel_id=1, source_target_pairs={{128,0},{129,1},{130,2},{131,3},{132,4},{133,5},{134,6},{135,7},{1... | collective-permute-start | bytes 884744 | tf_op jit(solution)/shard_map/ppermute | solution.py:21
  12.0 3.5 %copy-start.7 = (s32[32]{0:T(128)}, s32[32]{0:T(128)S(1)}, u32[]{:S(2)}) copy-start(s32[32]{0:T(128)S(1)} %add_add_fusion.slot_ref) | copy-start | bytes 388
  21.2 5.6 %copy-start.5 = (f32[7,7,192]{2,1,0:T(8,128)S(1)}, f32[7,7,192]{2,1,0:T(8,128)}, u32[]{:S(2)}) copy-start(f32[7,7,192]{2,1,0:T(8,128)} %param.12) | copy-start | bytes 112900
  21.2 6.6 %copy-start.2 = (bf16[1,16,256,192]{2,3,1,0:T(8,128)(2,1)S(1)}, bf16[1,16,256,192]{2,3,1,0:T(8,128)(2,1)}, u32[]{:S(2)}) copy-start(bf16[1,16,256,192]{2,3,1,0:T(8,128)(2,1)} %param.9) | copy-start | bytes 4718596
  21.2 77.5 %all-to-all-start.1 = ((bf16[16,3,192,128]{3,2,1,0:T(8,128)(2,1)}), bf16[16,3,192,128]{3,2,1,0:T(8,128)(2,1)}, u32[]{:S(2)}, u32[]{:S(2)}) async-start(bf16[16,3,192,128]{3,2,1,0:T(8,128)(2,1)} %broadcast_select_fusion), calls=%async_computation.1 | async-start | bytes 4718592 | tf_op jit(solution)/shard_map/all_to_all | solution.py:304
  61.6 0.7 copy-start.6
  94.5 1.2 copy-start.3
  98.6 29.1 %all-to-all-start = ((bf16[16,3,192,128]{3,2,1,0:T(8,128)(2,1)}), bf16[16,3,192,128]{3,2,1,0:T(8,128)(2,1)S(1)}, u32[]{:S(2)}, u32[]{:S(2)}) async-start(bf16[16,3,192,128]{3,2,1,0:T(8,128)(2,1)} %bitcast.111), calls=%async_computation | async-start | bytes 4718592 | tf_op jit(solution)/shard_map/all_to_all | solution.py:303
  146.8 6.2 %copy-start.4 = (bf16[4096,192]{0,1:T(8,128)(2,1)S(1)}, bf16[4096,192]{0,1:T(8,128)(2,1)}, u32[]{:S(2)}) copy-start(bf16[4096,192]{0,1:T(8,128)(2,1)} %copy-done.3) | copy-start | bytes 4718596
  146.8 149.4 %all-to-all-start.2 = ((bf16[8,6,192,128]{3,2,0,1:T(8,128)(2,1)}), bf16[8,6,192,128]{3,2,0,1:T(8,128)(2,1)}, u32[]{:S(2)}, u32[]{:S(2)}) async-start(bf16[8,6,192,128]{3,2,0,1:T(8,128)(2,1)} %copy.50), calls=%async_computation.2 | async-start | bytes 4718592 | tf_op jit(solution)/shard_map/all_to_all | solution.py:308
  303.2 5.0 %slice-start = ((s8[4718592]{0:T(1024)(128)(4,1)}), s8[4194304]{0:T(1024)(128)(4,1)S(1)}, s32[]{:S(2)}) async-start(s8[4718592]{0:T(1024)(128)(4,1)} %bitcast.120), calls=%async_computation.3 | async-start | bytes 8388608
  303.2 5.0 %slice-start.1 = ((s8[4718592]{0:T(1024)(128)(4,1)}), s8[524288]{0:T(1024)(128)(4,1)S(1)}, s32[]{:S(2)}) async-start(s8[4718592]{0:T(1024)(128)(4,1)} %bitcast.120), calls=%async_computation.4 | async-start | bytes 1048576
  303.2 7.2 %copy-start.1 = (bf16[768,192]{0,1:T(8,128)(2,1)S(1)}, bf16[768,192]{0,1:T(8,128)(2,1)}, u32[]{:S(2)}) copy-start(bf16[768,192]{0,1:T(8,128)(2,1)} %param.15) | copy-start | bytes 884740

commit v6 on v5

--- a/solution.py
+++ b/solution.py
@@ -225,6 +225,33 @@
     )(slot_of, dense_t, ret)
 
 
+def place_kernel(source_ref, filled_ref, src_ref, out_ref):
+    width = out_ref.shape[2]
+    per_row = src_ref.shape[2] // width
+    for s in range(out_ref.shape[0]):
+        b = source_ref[s]
+        row = src_ref[b // per_row]
+        k = b % per_row
+        piece = row[:, 0:width]
+        for j in range(1, per_row):
+            piece = jnp.where(k == j, row[:, j * width:(j + 1) * width], piece)
+        out_ref[s] = jnp.where(filled_ref[s] > 0, piece, jnp.zeros_like(piece))
+
+
+def place(block_of_slot, filled, src_t, width):
+    slots = block_of_slot.shape[0]
+    return pl.pallas_call(
+        place_kernel,
+        out_shape=jax.ShapeDtypeStruct((slots, src_t.shape[1], width), src_t.dtype),
+        in_specs=[
+            pl.BlockSpec(memory_space=pltpu.SMEM),
+            pl.BlockSpec(memory_space=pltpu.SMEM),
+            pl.BlockSpec(memory_space=pltpu.VMEM),
+        ],
+        out_specs=pl.BlockSpec(memory_space=pltpu.VMEM),
+    )(block_of_slot, filled, src_t)
+
+
 def gelu_slope(values):
     return (
         0.5 * (1.0 + lax.erf(values * 0.7071067811865476))
@@ -284,8 +311,6 @@
         pixels = pixels.reshape(rows, per_row, BLOCK, channels)
         return jnp.transpose(pixels, (0, 1, 3, 2)).reshape(rows * per_row, channels, BLOCK)
 
-    blocks = to_blocks(dense_out)
-    grad_blocks = to_blocks(cotangent)
     flat_labels = labels.reshape(-1)
     members = (flat_labels[:, None] == jnp.arange(EXPERTS, dtype=jnp.int32)[None, :]).astype(
         jnp.int32
@@ -295,10 +320,13 @@
     placer = jnp.arange(EXPERTS * CAP, dtype=jnp.int32)[:, None] == slot_of[None, :]
     block_of_slot = jnp.argmax(placer, axis=1)
     filled = jnp.any(placer, axis=1)[:, None, None]
-    outgoing = blocks[block_of_slot].reshape(EXPERTS, CAP, channels, BLOCK)
-    outgoing_grads = jnp.where(filled, grad_blocks[block_of_slot], jnp.zeros((), jnp.bfloat16)).reshape(
-        EXPERTS, CAP, channels, BLOCK
-    )
+    source = block_of_slot.astype(jnp.int32)
+    flags = filled.reshape(-1).astype(jnp.int32)
+    keep_all = jnp.ones_like(flags)
+    dense_t = jnp.transpose(dense_out.reshape(rows, width, channels), (0, 2, 1))
+    cot_t = jnp.transpose(cotangent.reshape(rows, width, channels), (0, 2, 1))
+    outgoing = place(source, keep_all, dense_t, BLOCK).reshape(EXPERTS, CAP, channels, BLOCK)
+    outgoing_grads = place(source, flags, cot_t, BLOCK).reshape(EXPERTS, CAP, channels, BLOCK)
     arrived, arrived_grads = (
         lax.all_to_all(outgoing, "exp", split_axis=0, concat_axis=1, tiled=True),
         lax.all_to_all(outgoing_grads, "exp", split_axis=0, concat_axis=1, tiled=True),
@@ -308,7 +336,6 @@
     returned = lax.all_to_all(results, "exp", split_axis=1, concat_axis=0, tiled=True)
     grad_in, grad_out_t = tree_allreduce(flat.reshape(-1, 128), local, channels, exp_in.shape[2])
     grad_out = jnp.transpose(grad_out_t, (0, 2, 1))
-    dense_t = jnp.transpose(dense_out.reshape(rows, width, channels), (0, 2, 1))
     out_t = assemble(slot_of.astype(jnp.int32), dense_t, returned.reshape(EXPERTS * CAP, channels, BLOCK))
     output = jnp.transpose(out_t, (0, 2, 1)).reshape(dense_out.shape)
     return (output, grad_in, grad_out)

time: 311 us -> 304 us (0.977)
  local copies, waits for them, and re-layouts: 33.4 us -> 23.6 us
  Pallas kernels: 163 us -> 170 us
  other arithmetic: 35.9 us -> 32.3 us
    pallas_call x0 -> x2, Pallas kernels: none -> 6.94 us  [place(): pl.pallas_call(place_kernel, out_shape=jax.ShapeDtypeStruct((slots, src_t...]
    gather x2 -> x0, local copies, waits for them, and re-layouts: 4.67 us -> none  [the longest x1 2.34 us: body(): grad_blocks[block_of_slot]]
    select_n x2 -> x0, other arithmetic: 3.3 us -> none  [the longest x1 3.29 us: body(): jnp.where(filled, grad_blocks[block_of_slot], jnp.zeros((), jnp.bfloat16))]
    unnamed x26 -> x24, local copies, waits for them, and re-layouts: 11.5 us -> 10.7 us
  transfers between devices with their start and end apart: 5 -> 5, of which waited for: 1 -> 1; matrix products, arithmetic and copies ran while one was open for 28% -> 24% of each run, Pallas kernels for 46% -> 49%
where the time goes in v6:
time: 304 us; the launch traced here: 303 us
  Pallas kernels  170 us (56%)
  other arithmetic  32.3 us (11%)
  matrix products  31.9 us (10%)
  local copies, waits for them, and re-layouts  23.6 us (8%)
  starting transfers between devices  22.3 us (7%)
  waiting for transfers between devices  22 us (7%)
    pallas_call x1, Pallas kernels, tree_allreduce(): pl.pallas_call(lambda *refs: allreduce_kernel(plan, rows, *refs), out_sha...  142 us
    dot_general x1, matrix products, dense_block(): reduced = jnp.dot(active, w_reduce, preferred_element_type=jnp.float32)  31.9 us
    reduce_sum x1, other arithmetic, dense_block(): channel_mean = jnp.mean(smoothed, axis=-1, keepdims=True)  26.9 us
    all_to_all x1, waiting for transfers between devices, body(): lax.all_to_all(outgoing, 'exp', split_axis=0, concat_axis=1, tiled=True)  22 us
    pallas_call x1, Pallas kernels, run_experts(): pl.pallas_call(expert_kernel, grid=(experts,), out_shape=[jax.ShapeDtypeS...  17.3 us
    unnamed x24, local copies, waits for them, and re-layouts  10.7 us
    pallas_call x2, Pallas kernels, place(): pl.pallas_call(place_kernel, out_shape=jax.ShapeDtypeStruct((slots, src_t...  6.94 us
  transfers between devices with their start and end apart: 5, of which 1 were waited for; matrix products, arithmetic and copies ran while one was open for 24% of the time, Pallas kernels for 49%

profile of v6, /device:TPU:7, one launch (start us, length us, event | category | flops | bytes accessed | tf_op | source)
XLA Modules:
  0.0 302.9 jit_solution(2734497334551358883)
XLA Ops:
  0.6 0.0 copy-start
  0.6 1.1 fusion.59
  1.8 1.3 collective-permute-start
  3.1 5.5 %collective-permute-start.1 = (bf16[1,3,256,192]{2,3,1,0:T(8,128)(2,1)S(1)}, bf16[1,3,256,192]{2,3,1,0:T(8,128)(2,1)S(1)}, u32[]{:S(2)}, u32[]{:S(2)}) collective-permute-start(bf16[1,3,256,192]{2,3,1,0:T(8,128)(2,1)S(1)} %get-tuple-element.19), channel_id=1, source_target_pairs={{128,0},{129,1},{130,2},{131,3},{132,4},{133,5},{134,6},{135,7},{1... | collective-permute-start | bytes 884744 | tf_op jit(solution)/shard_map/ppermute | solution.py:21
  8.6 0.8 copy.30
  9.4 0.1 reshape.216
  9.5 0.1 fusion.27
  9.5 0.1 reduce_window_sum.11
  9.6 0.2 select_reduce_fusion
  9.8 0.0 copy-start.5
  9.8 0.7 iota_reduce_fusion
  10.5 0.1 fusion.26
  10.6 0.5 convert_element_type.225.filled_ref
  11.1 3.5 %shard_map.113 = bf16[48,192,128]{2,1,0:T(8,128)(2,1)} custom-call(s32[48]{0:T(128)} %get-tuple-element.8.source_ref, s32[48]{0:T(128)} %convert_element_type.225.filled_ref, bf16[16,192,256]{2,1,0:T(8,128)(2,1)} %bitcast.114), custom_call_target="tpu_custom_call" | custom-call | tf_op jit(solution)/shard_map/pallas_call | solution.py:243
  14.6 0.0 copy-done.5
  14.6 5.6 %all-to-all-start.1 = ((bf16[16,3,192,128]{3,2,1,0:T(8,128)(2,1)}), bf16[16,3,192,128]{3,2,1,0:T(8,128)(2,1)}, u32[]{:S(2)}, u32[]{:S(2)}) async-start(bf16[16,3,192,128]{3,2,1,0:T(8,128)(2,1)} %bitcast.104), calls=%async_computation.1 | async-start | bytes 4718592 | tf_op jit(solution)/shard_map/all_to_all | solution.py:332
  20.2 0.0 collective-permute-done
  20.3 0.0 copy-done.2
  20.3 0.7 constant_dynamic-update-slice_fusion
  20.9 2.1 copy.39
  23.0 0.0 collective-permute-done.1
  23.0 2.2 fusion.25
  25.3 26.9 %fusion.58 = (f32[16,256]{1,0:T(8,128)S(1)}, f32[1,16,256,192]{2,3,1,0:T(8,128)S(1)}) fusion(f32[192]{0:T(256)S(1)} %bitcast.146, bf16[1,22,262,192]{2,3,1,0:T(8,128)(2,1)S(1)} %fusion.25, f32[192]{0:T(256)S(1)} %bitcast.147, f32[192]{0:T(256)S(1)} %bitcast.119, f32[192]{0:T(256)S(1)} %bitcast.120, ...), kind=kLoop, calls=%fused_computation.78 | loop fusion | flops 115601408 | bytes 80270080 | tf_op jit(solution)/shard_map/reduce_sum | solution.py:279
  52.2 0.0 copy-start.4
  52.2 0.3 multiply_reduce_fusion
  52.6 0.3 copy-done.4
  52.9 0.5 fusion.63
  53.4 0.2 copy.40
  53.6 0.0 copy-done
  53.6 0.2 copy-done.6
  53.8 31.9 %fusion.16 = bf16[4096,192]{0,1:T(8,128)(2,1)} fusion(f32[4096,192]{0,1:T(8,128)} %bitcast.112, bf16[768,192]{0,1:T(8,128)(2,1)S(1)} %copy-done, bf16[4096,192]{0,1:T(8,128)(2,1)S(1)} %bitcast.115, bf16[192,768]{1,0:T(8,128)(2,1)S(1)} %copy-done.6), kind=kOutput, calls=%fused_computation.24 | convolution fusion | flops 2621964288 | bytes 6881280 | tf_op jit(solution)/shard_map/dot_general | solution.py:286
  85.7 2.8 copy.44
  88.5 0.5 broadcast_in_dim.2.filled_ref
  89.0 3.5 %shard_map.112 = bf16[48,192,128]{2,1,0:T(8,128)(2,1)} custom-call(s32[48]{0:T(128)} %get-tuple-element.8.source_ref, s32[48]{0:T(128)} %broadcast_in_dim.2.filled_ref, bf16[16,192,256]{2,1,0:T(8,128)(2,1)} %bitcast.100), custom_call_target="tpu_custom_call" | custom-call | tf_op jit(solution)/shard_map/pallas_call | solution.py:243
  92.5 0.0 all-to-all-done.1
  92.5 3.8 %all-to-all-start = ((bf16[16,3,192,128]{3,2,1,0:T(8,128)(2,1)}), bf16[16,3,192,128]{3,2,1,0:T(8,128)(2,1)S(1)}, u32[]{:S(2)}, u32[]{:S(2)}) async-start(bf16[16,3,192,128]{3,2,1,0:T(8,128)(2,1)} %bitcast.105), calls=%async_computation | async-start | bytes 4718592 | tf_op jit(solution)/shard_map/all_to_all | solution.py:331
  96.3 3.3 %copy.35 = bf16[8,2,3,192,128]{4,3,2,1,0:T(8,128)(2,1)} copy(bf16[8,2,3,192,128]{4,3,2,0,1:T(8,128)(2,1)} %bitcast.58) | data formatting | bytes 4718592 | tf_op jit(solution)/shard_map/all_to_all | solution.py:332
  99.6 22.0 %all-to-all-done = bf16[16,3,192,128]{3,2,1,0:T(8,128)(2,1)S(1)} async-done(((bf16[16,3,192,128]{3,2,1,0:T(8,128)(2,1)}), bf16[16,3,192,128]{3,2,1,0:T(8,128)(2,1)S(1)}, u32[]{:S(2)}, u32[]{:S(2)}) %all-to-all-start) | async-done | bytes 2359328 | tf_op jit(solution)/shard_map/all_to_all | solution.py:331
  121.6 0.2 copy.34
  121.8 17.3 %shard_map.114 = (bf16[8,6,192,128]{3,2,1,0:T(8,128)(2,1)S(1)}, f32[8,2,6,192,128]{4,3,2,1,0:T(8,128)}) custom-call(bf16[8,6,192,128]{3,2,1,0:T(8,128)(2,1)S(1)} %bitcast.99, bf16[8,6,192,128]{3,2,1,0:T(8,128)(2,1)} %bitcast.108, bf16[8,192,768]{2,1,0:T(8,128)(2,1)} %win_ref.1, bf16[8,192,768]{2,1,0:T(8,128)(2,1)} %bitcast.113), custom_call_target="tpu_custom_call" | custom-call | tf_op jit(solution)/shard_map/pallas_call | solution.py:193
  139.1 1.6 copy.36
  140.7 6.0 %all-to-all-start.2 = ((bf16[8,6,192,128]{3,2,0,1:T(8,128)(2,1)}), bf16[8,6,192,128]{3,2,0,1:T(8,128)(2,1)}, u32[]{:S(2)}, u32[]{:S(2)}) async-start(bf16[8,6,192,128]{3,2,0,1:T(8,128)(2,1)} %copy.36), calls=%async_computation.2 | async-start | bytes 4718592 | tf_op jit(solution)/shard_map/all_to_all | solution.py:336
  146.7 142.1 %shard_map.116 = (f32[8,192,768]{2,1,0:T(8,128)}, f32[8,192,768]{2,1,0:T(8,128)}) custom-call(f32[18432,128]{1,0:T(8,128)} %bitcast.103), custom_call_target="tpu_custom_call" | custom-call | tf_op jit(solution)/shard_map/pallas_call | solution.py:153
  288.8 0.0 all-to-all-done.2
  288.8 3.2 %copy.37 = bf16[8,2,3,192,128]{4,3,2,0,1:T(8,128)(2,1)} copy(bf16[8,2,3,192,128]{4,3,0,2,1:T(8,128)(2,1)} %bitcast.61) | data formatting | bytes 4718592 | tf_op jit(solution)/shard_map/all_to_all | solution.py:336
  292.0 3.7 %shard_map.115 = bf16[16,192,256]{2,1,0:T(8,128)(2,1)} custom-call(s32[32]{0:T(128)} %copy-done.5, bf16[16,192,256]{2,1,0:T(8,128)(2,1)} %bitcast.101, bf16[48,192,128]{2,1,0:T(8,128)(2,1)} %bitcast.107), custom_call_target="tpu_custom_call" | custom-call | tf_op jit(solution)/shard_map/pallas_call | solution.py:216
  295.8 5.0 %copy.49 = f32[8,192,768]{2,1,0:T(8,128)} copy(f32[8,192,768]{2,1,0:T(8,128)} %get-tuple-element.73) | data formatting | bytes 9437184
  300.7 2.2 copy.50
  (19 shorter events, 0.1 us)
Async XLA Ops:
  0.6 53.0 %copy-start = (bf16[768,192]{0,1:T(8,128)(2,1)S(1)}, bf16[768,192]{0,1:T(8,128)(2,1)}, u32[]{:S(2)}) copy-start(bf16[768,192]{0,1:T(8,128)(2,1)} %param.15) | copy-start | bytes 884740
  1.8 18.4 %collective-permute-start = (bf16[1,3,256,192]{2,3,1,0:T(8,128)(2,1)S(1)}, bf16[1,3,256,192]{2,3,1,0:T(8,128)(2,1)S(1)}, u32[]{:S(2)}, u32[]{:S(2)}) collective-permute-start(bf16[1,3,256,192]{2,3,1,0:T(8,128)(2,1)S(1)} %get-tuple-element.18), channel_id=1, source_target_pairs={{0,128},{1,129},{2,130},{3,131},{4,132},{5,133},{6,134},{7,135},{8... | collective-permute-start | bytes 884744 | tf_op jit(solution)/shard_map/ppermute | solution.py:18
  3.1 19.9 %collective-permute-start.1 = (bf16[1,3,256,192]{2,3,1,0:T(8,128)(2,1)S(1)}, bf16[1,3,256,192]{2,3,1,0:T(8,128)(2,1)S(1)}, u32[]{:S(2)}, u32[]{:S(2)}) collective-permute-start(bf16[1,3,256,192]{2,3,1,0:T(8,128)(2,1)S(1)} %get-tuple-element.19), channel_id=1, source_target_pairs={{128,0},{129,1},{130,2},{131,3},{132,4},{133,5},{134,6},{135,7},{1... | collective-permute-start | bytes 884744 | tf_op jit(solution)/shard_map/ppermute | solution.py:21
  9.8 4.8 %copy-start.5 = (s32[32]{0:T(128)}, s32[32]{0:T(128)S(1)}, u32[]{:S(2)}) copy-start(s32[32]{0:T(128)S(1)} %add_add_fusion.slot_ref) | copy-start | bytes 388
  14.6 5.6 %copy-start.3 = (f32[7,7,192]{2,1,0:T(8,128)S(1)}, f32[7,7,192]{2,1,0:T(8,128)}, u32[]{:S(2)}) copy-start(f32[7,7,192]{2,1,0:T(8,128)} %param.12) | copy-start | bytes 112900
  14.6 5.7 %copy-start.2 = (bf16[1,16,256,192]{2,3,1,0:T(8,128)(2,1)S(1)}, bf16[1,16,256,192]{2,3,1,0:T(8,128)(2,1)}, u32[]{:S(2)}) copy-start(bf16[1,16,256,192]{2,3,1,0:T(8,128)(2,1)} %param.9) | copy-start | bytes 4718596
  14.6 77.9 %all-to-all-start.1 = ((bf16[16,3,192,128]{3,2,1,0:T(8,128)(2,1)}), bf16[16,3,192,128]{3,2,1,0:T(8,128)(2,1)}, u32[]{:S(2)}, u32[]{:S(2)}) async-start(bf16[16,3,192,128]{3,2,1,0:T(8,128)(2,1)} %bitcast.104), calls=%async_computation.1 | async-start | bytes 4718592 | tf_op jit(solution)/shard_map/all_to_all | solution.py:332
  52.2 0.7 copy-start.4
  52.9 1.0 copy-start.6
  92.5 29.1 %all-to-all-start = ((bf16[16,3,192,128]{3,2,1,0:T(8,128)(2,1)}), bf16[16,3,192,128]{3,2,1,0:T(8,128)(2,1)S(1)}, u32[]{:S(2)}, u32[]{:S(2)}) async-start(bf16[16,3,192,128]{3,2,1,0:T(8,128)(2,1)} %bitcast.105), calls=%async_computation | async-start | bytes 4718592 | tf_op jit(solution)/shard_map/all_to_all | solution.py:331
  140.7 148.1 %all-to-all-start.2 = ((bf16[8,6,192,128]{3,2,0,1:T(8,128)(2,1)}), bf16[8,6,192,128]{3,2,0,1:T(8,128)(2,1)}, u32[]{:S(2)}, u32[]{:S(2)}) async-start(bf16[8,6,192,128]{3,2,0,1:T(8,128)(2,1)} %copy.36), calls=%async_computation.2 | async-start | bytes 4718592 | tf_op jit(solution)/shard_map/all_to_all | solution.py:336
  295.7 5.0 %slice-start = ((s8[4718592]{0:T(1024)(128)(4,1)}), s8[4194304]{0:T(1024)(128)(4,1)S(1)}, s32[]{:S(2)}) async-start(s8[4718592]{0:T(1024)(128)(4,1)} %bitcast.109), calls=%async_computation.3 | async-start | bytes 8388608
  295.7 5.0 %slice-start.1 = ((s8[4718592]{0:T(1024)(128)(4,1)}), s8[524288]{0:T(1024)(128)(4,1)S(1)}, s32[]{:S(2)}) async-start(s8[4718592]{0:T(1024)(128)(4,1)} %bitcast.109), calls=%async_computation.4 | async-start | bytes 1048576
  295.8 7.2 %copy-start.1 = (bf16[768,192]{0,1:T(8,128)(2,1)S(1)}, bf16[768,192]{0,1:T(8,128)(2,1)}, u32[]{:S(2)}) copy-start(bf16[768,192]{0,1:T(8,128)(2,1)} %param.15) | copy-start | bytes 884740

commit v7 on v6

--- a/solution.py
+++ b/solution.py
@@ -162,18 +162,19 @@
     )(flat)
 
 def expert_kernel(x_ref, g_ref, win_ref, wout_ref, out_ref, flat_ref):
-    slots = x_ref.shape[0]
-    x_t = jnp.concatenate([x_ref[s] for s in range(slots)], axis=1)
-    g_t = jnp.concatenate([g_ref[s] for s in range(slots)], axis=1)
+    sources, per_source = x_ref.shape[0], x_ref.shape[1]
+    slots = sources * per_source
+    x_t = jnp.concatenate([x_ref[s // per_source, s % per_source] for s in range(slots)], axis=1)
+    g_t = jnp.concatenate([g_ref[s // per_source, s % per_source] for s in range(slots)], axis=1)
     w_out_t = wout_ref[...]
     pre = lax.dot_general(x_t, win_ref[...], (((0,), (0,)), ((), ())), preferred_element_type=jnp.float32)
     cdf = 0.5 * (1.0 + lax.erf(pre * 0.7071067811865476))
     hidden = (pre * cdf).astype(jnp.bfloat16)
     out_t = lax.dot_general(w_out_t, hidden, (((1,), (1,)), ((), ())), preferred_element_type=jnp.float32)
     out_t = out_t.astype(out_ref.dtype)
-    width = out_ref.shape[2]
+    width = out_ref.shape[3]
     for s in range(slots):
-        out_ref[s] = out_t[:, s * width:(s + 1) * width]
+        out_ref[s // per_source, s % per_source] = out_t[:, s * width:(s + 1) * width]
     grad_out_t = jnp.dot(g_t, hidden, preferred_element_type=jnp.float32)
     back = lax.dot_general(g_t, w_out_t, (((0,), (0,)), ((), ())), preferred_element_type=jnp.float32)
     slope = cdf + pre * jnp.exp(-0.5 * pre * pre) * 0.3989422804014327
@@ -185,10 +186,10 @@
 
 
 def run_experts(inputs, grads, w_in, w_out_t):
-    experts, slots, channels, width = inputs.shape
+    sources, experts, per_source, channels, width = inputs.shape
     hidden = w_in.shape[2]
     pieces = hidden // 128
-    tok = pl.BlockSpec((None, slots, channels, width), lambda e: (e, 0, 0, 0))
+    tok = pl.BlockSpec((sources, None, per_source, channels, width), lambda e: (0, e, 0, 0, 0))
     weight = pl.BlockSpec((None, channels, hidden), lambda e: (e, 0, 0))
     return pl.pallas_call(
         expert_kernel,
@@ -327,13 +328,15 @@
     cot_t = jnp.transpose(cotangent.reshape(rows, width, channels), (0, 2, 1))
     outgoing = place(source, keep_all, dense_t, BLOCK).reshape(EXPERTS, CAP, channels, BLOCK)
     outgoing_grads = place(source, flags, cot_t, BLOCK).reshape(EXPERTS, CAP, channels, BLOCK)
+    groups = lax.axis_size("exp")
+    local = EXPERTS // groups
+    by_group = (groups, local, CAP, channels, BLOCK)
     arrived, arrived_grads = (
-        lax.all_to_all(outgoing, "exp", split_axis=0, concat_axis=1, tiled=True),
-        lax.all_to_all(outgoing_grads, "exp", split_axis=0, concat_axis=1, tiled=True),
+        lax.all_to_all(outgoing.reshape(by_group), "exp", split_axis=0, concat_axis=0, tiled=True),
+        lax.all_to_all(outgoing_grads.reshape(by_group), "exp", split_axis=0, concat_axis=0, tiled=True),
     )
-    local = arrived.shape[0]
     results, flat = run_experts(arrived, arrived_grads, exp_in, jnp.transpose(exp_out, (0, 2, 1)))
-    returned = lax.all_to_all(results, "exp", split_axis=1, concat_axis=0, tiled=True)
+    returned = lax.all_to_all(results, "exp", split_axis=0, concat_axis=0, tiled=True)
     grad_in, grad_out_t = tree_allreduce(flat.reshape(-1, 128), local, channels, exp_in.shape[2])
     grad_out = jnp.transpose(grad_out_t, (0, 2, 1))
     out_t = assemble(slot_of.astype(jnp.int32), dense_t, returned.reshape(EXPERTS * CAP, channels, BLOCK))

time: 304 us -> 300 us (0.987)
  blocking collectives: 0 us -> 29.1 us
  waiting for transfers between devices: 22 us -> 0.01 us
  local copies, waits for them, and re-layouts: 23.6 us -> 16.7 us
  starting transfers between devices: 22.3 us -> 18.5 us
    all_to_all x0 -> x1, blocking collectives: none -> 29.1 us  [body(): lax.all_to_all(outgoing.reshape(by_group), 'exp', split_axis=0, concat_ax...]
    all_to_all x3 -> x2, waiting for transfers between devices: 22 us -> 0.01 us  [the longest x1 0.01 us: body(): lax.all_to_all(outgoing_grads.reshape(by_group), 'exp', split_axis=0, con...]
    all_to_all x3 -> x0, local copies, waits for them, and re-layouts: 6.69 us -> none  [the longest x1 3.27 us: body(): lax.all_to_all(outgoing_grads, 'exp', split_axis=0, concat_axis=1, tiled=...]
    all_to_all x3 -> x2, starting transfers between devices: 15.5 us -> 11.6 us  [the longest x1 6.08 us: body(): lax.all_to_all(results, 'exp', split_axis=0, concat_axis=0, tiled=True)]
  transfers between devices with their start and end apart: 5 -> 4, of which waited for: 1 -> 0; matrix products, arithmetic and copies ran while one was open for 24% -> 24% of each run, Pallas kernels for 49% -> 50%
where the time goes in v7:
time: 300 us; the launch traced here: 299 us
  Pallas kernels  170 us (57%)
  other arithmetic  32.3 us (11%)
  matrix products  31.7 us (11%)
  blocking collectives  29.1 us (10%)
  starting transfers between devices  18.5 us (6%)
  local copies, waits for them, and re-layouts  16.7 us (6%)
    pallas_call x1, Pallas kernels, tree_allreduce(): pl.pallas_call(lambda *refs: allreduce_kernel(plan, rows, *refs), out_sha...  142 us
    dot_general x1, matrix products, dense_block(): reduced = jnp.dot(active, w_reduce, preferred_element_type=jnp.float32)  31.7 us
    all_to_all x1, blocking collectives, body(): lax.all_to_all(outgoing.reshape(by_group), 'exp', split_axis=0, concat_ax...  29.1 us
    reduce_sum x1, other arithmetic, dense_block(): channel_mean = jnp.mean(smoothed, axis=-1, keepdims=True)  26.9 us
    pallas_call x1, Pallas kernels, run_experts(): pl.pallas_call(expert_kernel, grid=(experts,), out_shape=[jax.ShapeDtypeS...  17.5 us
    unnamed x24, local copies, waits for them, and re-layouts  12.2 us
    pallas_call x2, Pallas kernels, place(): pl.pallas_call(place_kernel, out_shape=jax.ShapeDtypeStruct((slots, src_t...  6.94 us
    all_to_all x1, starting transfers between devices, body(): lax.all_to_all(results, 'exp', split_axis=0, concat_axis=0, tiled=True)  6.08 us
  transfers between devices with their start and end apart: 4, of which 0 were waited for; matrix products, arithmetic and copies ran while one was open for 24% of the time, Pallas kernels for 50%

profile of v7, /device:TPU:7, one launch (start us, length us, event | category | flops | bytes accessed | tf_op | source)
XLA Modules:
  0.0 299.3 jit_solution(16605802175311422287)
XLA Ops:
  0.6 0.0 copy-start
  0.6 1.1 fusion.59
  1.8 1.3 collective-permute-start
  3.1 5.5 %collective-permute-start.1 = (bf16[1,3,256,192]{2,3,1,0:T(8,128)(2,1)S(1)}, bf16[1,3,256,192]{2,3,1,0:T(8,128)(2,1)S(1)}, u32[]{:S(2)}, u32[]{:S(2)}) collective-permute-start(bf16[1,3,256,192]{2,3,1,0:T(8,128)(2,1)S(1)} %get-tuple-element.19), channel_id=1, source_target_pairs={{128,0},{129,1},{130,2},{131,3},{132,4},{133,5},{134,6},{135,7},{1... | collective-permute-start | bytes 884744 | tf_op jit(solution)/shard_map/ppermute | solution.py:21
  8.6 0.8 copy.18
  9.4 0.1 reshape.209
  9.5 0.1 fusion.27
  9.5 0.1 reduce_window_sum.11
  9.6 0.2 select_reduce_fusion
  9.8 0.0 copy-start.6
  9.8 0.7 iota_reduce_fusion
  10.5 0.1 fusion.26
  10.6 0.5 convert_element_type.225.filled_ref
  11.1 3.5 %shard_map.113 = bf16[48,192,128]{2,1,0:T(8,128)(2,1)} custom-call(s32[48]{0:T(128)} %get-tuple-element.8.source_ref, s32[48]{0:T(128)} %convert_element_type.225.filled_ref, bf16[16,192,256]{2,1,0:T(8,128)(2,1)} %bitcast.99), custom_call_target="tpu_custom_call" | custom-call | tf_op jit(solution)/shard_map/pallas_call | solution.py:244
  14.6 0.0 copy-start.4
  14.6 0.0 copy-done.6
  14.6 5.6 %all-to-all-start.1 = ((bf16[2,8,3,192,128]{4,3,2,1,0:T(8,128)(2,1)}), bf16[2,8,3,192,128]{4,3,2,1,0:T(8,128)(2,1)}, u32[]{:S(2)}, u32[]{:S(2)}) async-start(bf16[2,8,3,192,128]{4,3,2,1,0:T(8,128)(2,1)} %bitcast.92), calls=%async_computation.1 | async-start | bytes 4718592 | tf_op jit(solution)/shard_map/all_to_all | solution.py:336
  20.1 0.0 copy-done.4
  20.2 0.0 collective-permute-done
  20.3 0.0 copy-done.2
  20.3 0.6 constant_dynamic-update-slice_fusion
  20.9 2.1 copy.23
  23.0 0.0 collective-permute-done.1
  23.0 2.2 fusion.25
  25.2 26.9 %fusion.58 = (f32[16,256]{1,0:T(8,128)S(1)}, f32[1,16,256,192]{2,3,1,0:T(8,128)S(1)}) fusion(f32[192]{0:T(256)S(1)} %bitcast.131, bf16[1,22,262,192]{2,3,1,0:T(8,128)(2,1)S(1)} %fusion.25, f32[192]{0:T(256)S(1)} %bitcast.132, f32[192]{0:T(256)S(1)} %bitcast.104, f32[192]{0:T(256)S(1)} %bitcast.105, ...), kind=kLoop, calls=%fused_computation.78 | loop fusion | flops 115601408 | bytes 80270080 | tf_op jit(solution)/shard_map/reduce_sum | solution.py:280
  52.1 0.0 copy-start.5
  52.2 0.3 multiply_reduce_fusion
  52.5 0.3 copy-done.5
  52.8 0.5 fusion.63
  53.4 1.3 copy.24
  54.7 0.0 copy-done
  54.7 0.5 copy-done.3
  55.2 31.7 %fusion.16 = bf16[4096,192]{0,1:T(8,128)(2,1)} fusion(f32[4096,192]{0,1:T(8,128)S(1)} %bitcast.97, bf16[768,192]{0,1:T(8,128)(2,1)S(1)} %copy-done, bf16[4096,192]{0,1:T(8,128)(2,1)} %bitcast.100, bf16[192,768]{1,0:T(8,128)(2,1)} %param.14), kind=kOutput, calls=%fused_computation.24 | convolution fusion | flops 2621964288 | bytes 6881280 | tf_op jit(solution)/shard_map/dot_general | solution.py:287
  86.9 2.8 copy.28
  89.6 0.5 broadcast_in_dim.2.filled_ref
  90.1 3.5 %shard_map.112 = bf16[48,192,128]{2,1,0:T(8,128)(2,1)} custom-call(s32[48]{0:T(128)} %get-tuple-element.8.source_ref, s32[48]{0:T(128)} %broadcast_in_dim.2.filled_ref, bf16[16,192,256]{2,1,0:T(8,128)(2,1)} %bitcast.88), custom_call_target="tpu_custom_call" | custom-call | tf_op jit(solution)/shard_map/pallas_call | solution.py:244
  93.6 0.0 all-to-all-done.1.g_ref
  93.6 29.1 %all_to_all.15.x_ref = bf16[2,8,3,192,128]{4,3,2,1,0:T(8,128)(2,1)S(1)} all-to-all(bf16[2,8,3,192,128]{4,3,2,1,0:T(8,128)(2,1)} %bitcast.93), channel_id=1, replica_groups=mesh['lat'=2,'dp'=64,'exp'=2] {'exp'}, dimensions={0} | all-to-all | bytes 4718592 | tf_op jit(solution)/shard_map/all_to_all | solution.py:335
  122.7 17.5 %shard_map.114 = (bf16[2,8,3,192,128]{4,3,2,1,0:T(8,128)(2,1)}, f32[8,2,6,192,128]{4,3,2,1,0:T(8,128)}) custom-call(bf16[2,8,3,192,128]{4,3,2,1,0:T(8,128)(2,1)S(1)} %all_to_all.15.x_ref, bf16[2,8,3,192,128]{4,3,2,1,0:T(8,128)(2,1)} %all-to-all-done.1.g_ref, bf16[8,192,768]{2,1,0:T(8,128)(2,1)} %win_ref.1, bf16[8,192,768]{2,1,0:T(8,128)(2,1)} %bitcast.98), custom_call_target="tpu_custom_call" | custom-call | tf_op jit(solution)/shard_map/pallas_call | solution.py:194
  140.2 6.1 %all-to-all-start.2 = ((bf16[2,8,3,192,128]{4,3,2,1,0:T(8,128)(2,1)}), bf16[2,8,3,192,128]{4,3,2,1,0:T(8,128)(2,1)}, u32[]{:S(2)}, u32[]{:S(2)}) async-start(bf16[2,8,3,192,128]{4,3,2,1,0:T(8,128)(2,1)} %get-tuple-element.9), calls=%async_computation.2 | async-start | bytes 4718592 | tf_op jit(solution)/shard_map/all_to_all | solution.py:339
  146.3 142.1 %shard_map.116 = (f32[8,192,768]{2,1,0:T(8,128)}, f32[8,192,768]{2,1,0:T(8,128)}) custom-call(f32[18432,128]{1,0:T(8,128)} %bitcast.91), custom_call_target="tpu_custom_call" | custom-call | tf_op jit(solution)/shard_map/pallas_call | solution.py:153
  288.4 0.0 all-to-all-done.2
  288.4 3.7 %shard_map.115 = bf16[16,192,256]{2,1,0:T(8,128)(2,1)} custom-call(s32[32]{0:T(128)} %copy-done.6, bf16[16,192,256]{2,1,0:T(8,128)(2,1)} %bitcast.89, bf16[48,192,128]{2,1,0:T(8,128)(2,1)} %bitcast.55.ret_ref), custom_call_target="tpu_custom_call" | custom-call | tf_op jit(solution)/shard_map/pallas_call | solution.py:217
  292.1 5.0 %copy.33 = f32[8,192,768]{2,1,0:T(8,128)} copy(f32[8,192,768]{2,1,0:T(8,128)} %get-tuple-element.73) | data formatting | bytes 9437184
  297.1 0.0 slice-done
  297.1 0.0 slice-done.1
  297.1 2.2 copy.34
  299.3 0.0 copy-done.1
  (14 shorter events, 0.1 us)
Async XLA Ops:
  0.6 54.1 %copy-start = (bf16[768,192]{0,1:T(8,128)(2,1)S(1)}, bf16[768,192]{0,1:T(8,128)(2,1)}, u32[]{:S(2)}) copy-start(bf16[768,192]{0,1:T(8,128)(2,1)} %param.15) | copy-start | bytes 884740
  1.8 18.4 %collective-permute-start = (bf16[1,3,256,192]{2,3,1,0:T(8,128)(2,1)S(1)}, bf16[1,3,256,192]{2,3,1,0:T(8,128)(2,1)S(1)}, u32[]{:S(2)}, u32[]{:S(2)}) collective-permute-start(bf16[1,3,256,192]{2,3,1,0:T(8,128)(2,1)S(1)} %get-tuple-element.18), channel_id=1, source_target_pairs={{0,128},{1,129},{2,130},{3,131},{4,132},{5,133},{6,134},{7,135},{8... | collective-permute-start | bytes 884744 | tf_op jit(solution)/shard_map/ppermute | solution.py:18
  3.1 19.9 %collective-permute-start.1 = (bf16[1,3,256,192]{2,3,1,0:T(8,128)(2,1)S(1)}, bf16[1,3,256,192]{2,3,1,0:T(8,128)(2,1)S(1)}, u32[]{:S(2)}, u32[]{:S(2)}) collective-permute-start(bf16[1,3,256,192]{2,3,1,0:T(8,128)(2,1)S(1)} %get-tuple-element.19), channel_id=1, source_target_pairs={{128,0},{129,1},{130,2},{131,3},{132,4},{133,5},{134,6},{135,7},{1... | collective-permute-start | bytes 884744 | tf_op jit(solution)/shard_map/ppermute | solution.py:21
  9.8 4.8 %copy-start.6 = (s32[32]{0:T(128)}, s32[32]{0:T(128)S(1)}, u32[]{:S(2)}) copy-start(s32[32]{0:T(128)S(1)} %add_add_fusion.slot_ref) | copy-start | bytes 388
  14.6 5.6 %copy-start.4 = (f32[7,7,192]{2,1,0:T(8,128)S(1)}, f32[7,7,192]{2,1,0:T(8,128)}, u32[]{:S(2)}) copy-start(f32[7,7,192]{2,1,0:T(8,128)} %param.12) | copy-start | bytes 112900
  14.6 5.7 %copy-start.2 = (bf16[1,16,256,192]{2,3,1,0:T(8,128)(2,1)S(1)}, bf16[1,16,256,192]{2,3,1,0:T(8,128)(2,1)}, u32[]{:S(2)}) copy-start(bf16[1,16,256,192]{2,3,1,0:T(8,128)(2,1)} %param.9) | copy-start | bytes 4718596
  14.6 79.0 %all-to-all-start.1 = ((bf16[2,8,3,192,128]{4,3,2,1,0:T(8,128)(2,1)}), bf16[2,8,3,192,128]{4,3,2,1,0:T(8,128)(2,1)}, u32[]{:S(2)}, u32[]{:S(2)}) async-start(bf16[2,8,3,192,128]{4,3,2,1,0:T(8,128)(2,1)} %bitcast.92), calls=%async_computation.1 | async-start | bytes 4718592 | tf_op jit(solution)/shard_map/all_to_all | solution.py:336
  52.1 0.7 copy-start.5
  52.8 2.4 copy-start.3
  140.2 148.2 %all-to-all-start.2 = ((bf16[2,8,3,192,128]{4,3,2,1,0:T(8,128)(2,1)}), bf16[2,8,3,192,128]{4,3,2,1,0:T(8,128)(2,1)}, u32[]{:S(2)}, u32[]{:S(2)}) async-start(bf16[2,8,3,192,128]{4,3,2,1,0:T(8,128)(2,1)} %get-tuple-element.9), calls=%async_computation.2 | async-start | bytes 4718592 | tf_op jit(solution)/shard_map/all_to_all | solution.py:339
  292.1 5.0 %slice-start = ((s8[4718592]{0:T(1024)(128)(4,1)}), s8[4194304]{0:T(1024)(128)(4,1)S(1)}, s32[]{:S(2)}) async-start(s8[4718592]{0:T(1024)(128)(4,1)} %bitcast.94), calls=%async_computation.3 | async-start | bytes 8388608
  292.1 5.0 %slice-start.1 = ((s8[4718592]{0:T(1024)(128)(4,1)}), s8[524288]{0:T(1024)(128)(4,1)S(1)}, s32[]{:S(2)}) async-start(s8[4718592]{0:T(1024)(128)(4,1)} %bitcast.94), calls=%async_computation.4 | async-start | bytes 1048576
  292.1 7.2 %copy-start.1 = (bf16[768,192]{0,1:T(8,128)(2,1)S(1)}, bf16[768,192]{0,1:T(8,128)(2,1)}, u32[]{:S(2)}) copy-start(bf16[768,192]{0,1:T(8,128)(2,1)} %param.15) | copy-start | bytes 884740

commit v8 on v7

--- a/solution.py
+++ b/solution.py
@@ -79,7 +79,7 @@
                 pl.ds(at, chunk)
             ].astype(jnp.float32)
 
-        parts = 2 if half >= 576 else 1
+        parts = 4 if half >= 4608 else (2 if half >= 576 else 1)
         piece = half // parts
         copies = []
         for p in range(parts):
@@ -95,8 +95,8 @@
             copy = pltpu.make_async_remote_copy(
                 src_ref=staged[k].at[pl.ds(p * piece, piece)],
                 dst_ref=bufs[k].at[pl.ds(p * piece, piece)],
-                send_sem=rs_send.at[2 * k + p],
-                recv_sem=rs_recv.at[2 * k + p],
+                send_sem=rs_send.at[4 * k + p],
+                recv_sem=rs_recv.at[4 * k + p],
                 device_id=partners[k],
                 device_id_type=pl.DeviceIdType.MESH,
             )
@@ -149,7 +149,7 @@
     scratch += [pltpu.VMEM((rows >> (k + 1), 128), jnp.float32) for k in range(stages)]
     scratch += [pltpu.VMEM((rows >> (k + 1), 128), jnp.bfloat16) for k in range(stages)]
     scratch += [pltpu.VMEM((rows, 128), jnp.bfloat16)]
-    scratch += [pltpu.SemaphoreType.DMA((2 * stages,))] * 2 + [pltpu.SemaphoreType.DMA((stages,))] * 2
+    scratch += [pltpu.SemaphoreType.DMA((4 * stages,))] * 2 + [pltpu.SemaphoreType.DMA((stages,))] * 2
     return pl.pallas_call(
         lambda *refs: allreduce_kernel(plan, rows, *refs),
         out_shape=[jax.ShapeDtypeStruct((experts, channels, hidden), jnp.float32)] * 2,

time: 300 us -> 300 us (level)
  no operation moved by 1% of the time
where the time goes in v8:
time: 300 us; the launch traced here: 299 us
  Pallas kernels  170 us (57%)
  other arithmetic  32.3 us (11%)
  matrix products  31.7 us (11%)
  blocking collectives  29.1 us (10%)
  starting transfers between devices  18.5 us (6%)
  local copies, waits for them, and re-layouts  16.7 us (6%)
    pallas_call x1, Pallas kernels, tree_allreduce(): pl.pallas_call(lambda *refs: allreduce_kernel(plan, rows, *refs), out_sha...  142 us
    dot_general x1, matrix products, dense_block(): reduced = jnp.dot(active, w_reduce, preferred_element_type=jnp.float32)  31.7 us
    all_to_all x1, blocking collectives, body(): lax.all_to_all(outgoing.reshape(by_group), 'exp', split_axis=0, concat_ax...  29.1 us
    reduce_sum x1, other arithmetic, dense_block(): channel_mean = jnp.mean(smoothed, axis=-1, keepdims=True)  26.9 us
    pallas_call x1, Pallas kernels, run_experts(): pl.pallas_call(expert_kernel, grid=(experts,), out_shape=[jax.ShapeDtypeS...  17.5 us
    unnamed x24, local copies, waits for them, and re-layouts  12.2 us
    pallas_call x2, Pallas kernels, place(): pl.pallas_call(place_kernel, out_shape=jax.ShapeDtypeStruct((slots, src_t...  6.94 us
    all_to_all x1, starting transfers between devices, body(): lax.all_to_all(results, 'exp', split_axis=0, concat_axis=0, tiled=True)  6.08 us
  transfers between devices with their start and end apart: 4, of which 0 were waited for; matrix products, arithmetic and copies ran while one was open for 24% of the time, Pallas kernels for 50%

profile of v8, /device:TPU:7, one launch (start us, length us, event | category | flops | bytes accessed | tf_op | source)
XLA Modules:
  0.0 299.3 jit_solution(16826235096469810100)
XLA Ops:
  0.6 0.0 copy-start
  0.6 1.1 fusion.59
  1.8 1.3 collective-permute-start
  3.1 5.5 %collective-permute-start.1 = (bf16[1,3,256,192]{2,3,1,0:T(8,128)(2,1)S(1)}, bf16[1,3,256,192]{2,3,1,0:T(8,128)(2,1)S(1)}, u32[]{:S(2)}, u32[]{:S(2)}) collective-permute-start(bf16[1,3,256,192]{2,3,1,0:T(8,128)(2,1)S(1)} %get-tuple-element.19), channel_id=1, source_target_pairs={{128,0},{129,1},{130,2},{131,3},{132,4},{133,5},{134,6},{135,7},{1... | collective-permute-start | bytes 884744 | tf_op jit(solution)/shard_map/ppermute | solution.py:21
  8.6 0.8 copy.18
  9.4 0.1 reshape.209
  9.5 0.1 fusion.27
  9.5 0.1 reduce_window_sum.11
  9.6 0.2 select_reduce_fusion
  9.8 0.0 copy-start.6
  9.8 0.7 iota_reduce_fusion
  10.5 0.1 fusion.26
  10.6 0.5 convert_element_type.225.filled_ref
  11.1 3.5 %shard_map.113 = bf16[48,192,128]{2,1,0:T(8,128)(2,1)} custom-call(s32[48]{0:T(128)} %get-tuple-element.8.source_ref, s32[48]{0:T(128)} %convert_element_type.225.filled_ref, bf16[16,192,256]{2,1,0:T(8,128)(2,1)} %bitcast.99), custom_call_target="tpu_custom_call" | custom-call | tf_op jit(solution)/shard_map/pallas_call | solution.py:244
  14.6 0.0 copy-start.4
  14.6 0.0 copy-done.6
  14.6 5.6 %all-to-all-start.1 = ((bf16[2,8,3,192,128]{4,3,2,1,0:T(8,128)(2,1)}), bf16[2,8,3,192,128]{4,3,2,1,0:T(8,128)(2,1)}, u32[]{:S(2)}, u32[]{:S(2)}) async-start(bf16[2,8,3,192,128]{4,3,2,1,0:T(8,128)(2,1)} %bitcast.92), calls=%async_computation.1 | async-start | bytes 4718592 | tf_op jit(solution)/shard_map/all_to_all | solution.py:336
  20.1 0.0 copy-done.4
  20.2 0.0 collective-permute-done
  20.3 0.0 copy-done.2
  20.3 0.6 constant_dynamic-update-slice_fusion
  20.9 2.1 copy.23
  23.0 0.0 collective-permute-done.1
  23.0 2.2 fusion.25
  25.2 26.9 %fusion.58 = (f32[16,256]{1,0:T(8,128)S(1)}, f32[1,16,256,192]{2,3,1,0:T(8,128)S(1)}) fusion(f32[192]{0:T(256)S(1)} %bitcast.131, bf16[1,22,262,192]{2,3,1,0:T(8,128)(2,1)S(1)} %fusion.25, f32[192]{0:T(256)S(1)} %bitcast.132, f32[192]{0:T(256)S(1)} %bitcast.104, f32[192]{0:T(256)S(1)} %bitcast.105, ...), kind=kLoop, calls=%fused_computation.78 | loop fusion | flops 115601408 | bytes 80270080 | tf_op jit(solution)/shard_map/reduce_sum | solution.py:280
  52.1 0.0 copy-start.5
  52.2 0.3 multiply_reduce_fusion
  52.5 0.3 copy-done.5
  52.8 0.5 fusion.63
  53.4 1.3 copy.24
  54.7 0.0 copy-done
  54.7 0.5 copy-done.3
  55.2 31.7 %fusion.16 = bf16[4096,192]{0,1:T(8,128)(2,1)} fusion(f32[4096,192]{0,1:T(8,128)S(1)} %bitcast.97, bf16[768,192]{0,1:T(8,128)(2,1)S(1)} %copy-done, bf16[4096,192]{0,1:T(8,128)(2,1)} %bitcast.100, bf16[192,768]{1,0:T(8,128)(2,1)} %param.14), kind=kOutput, calls=%fused_computation.24 | convolution fusion | flops 2621964288 | bytes 6881280 | tf_op jit(solution)/shard_map/dot_general | solution.py:287
  86.9 2.8 copy.28
  89.6 0.5 broadcast_in_dim.2.filled_ref
  90.1 3.5 %shard_map.112 = bf16[48,192,128]{2,1,0:T(8,128)(2,1)} custom-call(s32[48]{0:T(128)} %get-tuple-element.8.source_ref, s32[48]{0:T(128)} %broadcast_in_dim.2.filled_ref, bf16[16,192,256]{2,1,0:T(8,128)(2,1)} %bitcast.88), custom_call_target="tpu_custom_call" | custom-call | tf_op jit(solution)/shard_map/pallas_call | solution.py:244
  93.6 0.0 all-to-all-done.1.g_ref
  93.6 29.1 %all_to_all.15.x_ref = bf16[2,8,3,192,128]{4,3,2,1,0:T(8,128)(2,1)S(1)} all-to-all(bf16[2,8,3,192,128]{4,3,2,1,0:T(8,128)(2,1)} %bitcast.93), channel_id=1, replica_groups=mesh['lat'=2,'dp'=64,'exp'=2] {'exp'}, dimensions={0} | all-to-all | bytes 4718592 | tf_op jit(solution)/shard_map/all_to_all | solution.py:335
  122.7 17.5 %shard_map.114 = (bf16[2,8,3,192,128]{4,3,2,1,0:T(8,128)(2,1)}, f32[8,2,6,192,128]{4,3,2,1,0:T(8,128)}) custom-call(bf16[2,8,3,192,128]{4,3,2,1,0:T(8,128)(2,1)S(1)} %all_to_all.15.x_ref, bf16[2,8,3,192,128]{4,3,2,1,0:T(8,128)(2,1)} %all-to-all-done.1.g_ref, bf16[8,192,768]{2,1,0:T(8,128)(2,1)} %win_ref.1, bf16[8,192,768]{2,1,0:T(8,128)(2,1)} %bitcast.98), custom_call_target="tpu_custom_call" | custom-call | tf_op jit(solution)/shard_map/pallas_call | solution.py:194
  140.2 6.1 %all-to-all-start.2 = ((bf16[2,8,3,192,128]{4,3,2,1,0:T(8,128)(2,1)}), bf16[2,8,3,192,128]{4,3,2,1,0:T(8,128)(2,1)}, u32[]{:S(2)}, u32[]{:S(2)}) async-start(bf16[2,8,3,192,128]{4,3,2,1,0:T(8,128)(2,1)} %get-tuple-element.9), calls=%async_computation.2 | async-start | bytes 4718592 | tf_op jit(solution)/shard_map/all_to_all | solution.py:339
  146.3 142.1 %shard_map.116 = (f32[8,192,768]{2,1,0:T(8,128)}, f32[8,192,768]{2,1,0:T(8,128)}) custom-call(f32[18432,128]{1,0:T(8,128)} %bitcast.91), custom_call_target="tpu_custom_call" | custom-call | tf_op jit(solution)/shard_map/pallas_call | solution.py:153
  288.4 0.0 all-to-all-done.2
  288.4 3.7 %shard_map.115 = bf16[16,192,256]{2,1,0:T(8,128)(2,1)} custom-call(s32[32]{0:T(128)} %copy-done.6, bf16[16,192,256]{2,1,0:T(8,128)(2,1)} %bitcast.89, bf16[48,192,128]{2,1,0:T(8,128)(2,1)} %bitcast.55.ret_ref), custom_call_target="tpu_custom_call" | custom-call | tf_op jit(solution)/shard_map/pallas_call | solution.py:217
  292.1 5.0 %copy.33 = f32[8,192,768]{2,1,0:T(8,128)} copy(f32[8,192,768]{2,1,0:T(8,128)} %get-tuple-element.73) | data formatting | bytes 9437184
  297.1 0.0 slice-done
  297.1 0.0 slice-done.1
  297.1 2.2 copy.34
  299.3 0.0 copy-done.1
  (14 shorter events, 0.1 us)
Async XLA Ops:
  0.6 54.1 %copy-start = (bf16[768,192]{0,1:T(8,128)(2,1)S(1)}, bf16[768,192]{0,1:T(8,128)(2,1)}, u32[]{:S(2)}) copy-start(bf16[768,192]{0,1:T(8,128)(2,1)} %param.15) | copy-start | bytes 884740
  1.8 18.4 %collective-permute-start = (bf16[1,3,256,192]{2,3,1,0:T(8,128)(2,1)S(1)}, bf16[1,3,256,192]{2,3,1,0:T(8,128)(2,1)S(1)}, u32[]{:S(2)}, u32[]{:S(2)}) collective-permute-start(bf16[1,3,256,192]{2,3,1,0:T(8,128)(2,1)S(1)} %get-tuple-element.18), channel_id=1, source_target_pairs={{0,128},{1,129},{2,130},{3,131},{4,132},{5,133},{6,134},{7,135},{8... | collective-permute-start | bytes 884744 | tf_op jit(solution)/shard_map/ppermute | solution.py:18
  3.1 19.9 %collective-permute-start.1 = (bf16[1,3,256,192]{2,3,1,0:T(8,128)(2,1)S(1)}, bf16[1,3,256,192]{2,3,1,0:T(8,128)(2,1)S(1)}, u32[]{:S(2)}, u32[]{:S(2)}) collective-permute-start(bf16[1,3,256,192]{2,3,1,0:T(8,128)(2,1)S(1)} %get-tuple-element.19), channel_id=1, source_target_pairs={{128,0},{129,1},{130,2},{131,3},{132,4},{133,5},{134,6},{135,7},{1... | collective-permute-start | bytes 884744 | tf_op jit(solution)/shard_map/ppermute | solution.py:21
  9.8 4.8 %copy-start.6 = (s32[32]{0:T(128)}, s32[32]{0:T(128)S(1)}, u32[]{:S(2)}) copy-start(s32[32]{0:T(128)S(1)} %add_add_fusion.slot_ref) | copy-start | bytes 388
  14.6 5.6 %copy-start.4 = (f32[7,7,192]{2,1,0:T(8,128)S(1)}, f32[7,7,192]{2,1,0:T(8,128)}, u32[]{:S(2)}) copy-start(f32[7,7,192]{2,1,0:T(8,128)} %param.12) | copy-start | bytes 112900
  14.6 5.7 %copy-start.2 = (bf16[1,16,256,192]{2,3,1,0:T(8,128)(2,1)S(1)}, bf16[1,16,256,192]{2,3,1,0:T(8,128)(2,1)}, u32[]{:S(2)}) copy-start(bf16[1,16,256,192]{2,3,1,0:T(8,128)(2,1)} %param.9) | copy-start | bytes 4718596
  14.6 79.0 %all-to-all-start.1 = ((bf16[2,8,3,192,128]{4,3,2,1,0:T(8,128)(2,1)}), bf16[2,8,3,192,128]{4,3,2,1,0:T(8,128)(2,1)}, u32[]{:S(2)}, u32[]{:S(2)}) async-start(bf16[2,8,3,192,128]{4,3,2,1,0:T(8,128)(2,1)} %bitcast.92), calls=%async_computation.1 | async-start | bytes 4718592 | tf_op jit(solution)/shard_map/all_to_all | solution.py:336
  52.1 0.7 copy-start.5
  52.8 2.4 copy-start.3
  140.2 148.2 %all-to-all-start.2 = ((bf16[2,8,3,192,128]{4,3,2,1,0:T(8,128)(2,1)}), bf16[2,8,3,192,128]{4,3,2,1,0:T(8,128)(2,1)}, u32[]{:S(2)}, u32[]{:S(2)}) async-start(bf16[2,8,3,192,128]{4,3,2,1,0:T(8,128)(2,1)} %get-tuple-element.9), calls=%async_computation.2 | async-start | bytes 4718592 | tf_op jit(solution)/shard_map/all_to_all | solution.py:339
  292.1 5.0 %slice-start = ((s8[4718592]{0:T(1024)(128)(4,1)}), s8[4194304]{0:T(1024)(128)(4,1)S(1)}, s32[]{:S(2)}) async-start(s8[4718592]{0:T(1024)(128)(4,1)} %bitcast.94), calls=%async_computation.3 | async-start | bytes 8388608
  292.1 5.0 %slice-start.1 = ((s8[4718592]{0:T(1024)(128)(4,1)}), s8[524288]{0:T(1024)(128)(4,1)S(1)}, s32[]{:S(2)}) async-start(s8[4718592]{0:T(1024)(128)(4,1)} %bitcast.94), calls=%async_computation.4 | async-start | bytes 1048576
  292.1 7.2 %copy-start.1 = (bf16[768,192]{0,1:T(8,128)(2,1)S(1)}, bf16[768,192]{0,1:T(8,128)(2,1)}, u32[]{:S(2)}) copy-start(bf16[768,192]{0,1:T(8,128)(2,1)} %param.15) | copy-start | bytes 884740
